TPU v7x, 32 devices: a whole 2x2x4 slice. The times are simulated.
32 devices in a mesh: dp: 8 (over y, x, core), tensor: 4 (over z).
Axes of the slice: x: 2, y: 2, z: 4, core: 2. Of those that a mesh axis runs over, the one named last changes fastest.
Arguments:
- hidden: bfloat16 [8, 1280, 1120], P('dp', 'tensor'), may hold values from -6 to 6
- segment_ids: int32 [8, 1280], P('dp'), may hold values from 0 to 15, as said below
- lengths: int32 [8], P('dp'), may hold values from 640 to 1280, as said below
- norm1_gain: float32 [1120], replicated, may hold values from 0.25 to 1.75
- norm1_shift: float32 [1120], replicated, may hold values from -4 to 4
- qkv_weight: bfloat16 [3, 1120, 1120], P(None, None, 'tensor'), may hold values from -0.1875 to 0.1875
- qv_bias: float32 [2, 1120], P(None, 'tensor'), may hold values from -4 to 4
- out_weight: bfloat16 [1120, 1120], P('tensor'), may hold values from -1 to 1
- out_bias: float32 [1120], replicated, may hold values from -4 to 4
- norm2_gain: float32 [1120], replicated, may hold values from 0.25 to 1.75
- norm2_shift: float32 [1120], replicated, may hold values from -4 to 4
- up_weight: bfloat16 [1120, 4480], P(None, 'tensor'), may hold values from -0.1875 to 0.1875
- up_bias: float32 [4480], P('tensor'), may hold values from -4 to 4
- down_weight: bfloat16 [4480, 1120], P('tensor'), may hold values from -0.125 to 0.125
- down_bias: float32 [1120], replicated, may hold values from -4 to 4
- cotangent: bfloat16 [8, 1280, 1120], P('dp', 'tensor'), may hold values from -6 to 6
Outputs:
- output: bfloat16 [8, 1280, 1120], P('dp', 'tensor')
- input_grad: bfloat16 [8, 1280, 1120], P('dp', 'tensor')
- norm1_gain_grad: float32 [1120], replicated
- norm1_shift_grad: float32 [1120], replicated
- qkv_weight_grad: float32 [3, 1120, 1120], P(None, None, 'tensor')
- qv_bias_grad: float32 [2, 1120], P(None, 'tensor')
- out_weight_grad: float32 [1120, 1120], P('tensor')
- out_bias_grad: float32 [1120], replicated
- norm2_gain_grad: float32 [1120], replicated
- norm2_shift_grad: float32 [1120], replicated
- up_weight_grad: float32 [1120, 4480], P(None, 'tensor')
- up_bias_grad: float32 [4480], P('tensor')
- down_weight_grad: float32 [4480, 1120], P('tensor')
- down_bias_grad: float32 [1120], replicated
Inputs may be any that keep to these rules, and one draw needn't show every extreme that they name: `segment_ids`: along each row the ids start at 0 and never fall; a cell is a run of equal ids. `lengths`: some row is full and some row holds 640 live tokens.
All inputs are finite; a program needn't handle non-finite values.
Results may differ from a plain program's by a relative error of at most 0.012.
Values may be sent and summed in bfloat16 or wider, within the bound.
A program may use at most 256 MiB of HBM per device.

v0:
```python
import jax
import jax.numpy as jnp
from jax import lax
from jax.sharding import PartitionSpec as P

HEAD = 56


EPS = 1e-05


def norm_rows(values, gain, shift):
    center = values - jnp.mean(values, axis=-1, keepdims=True)
    spread = jnp.mean(center * center, axis=-1, keepdims=True)
    return center * lax.rsqrt(spread + EPS) * gain + shift


def row_mask(segment, length):
    places = jnp.arange(segment.shape[0], dtype=jnp.int32)
    earlier = places[None, :] <= places[:, None]
    live = places < length
    same = (segment[:, None] == segment[None, :]) & live[:, None] & live[None, :]
    return earlier & (same | (places[:, None] == places[None, :]))


def masked_scores(query_row, key_row, segment, length, scale):
    scores = (
        jnp.einsum("qhe,khe->hqk", query_row, key_row, preferred_element_type=jnp.float32) * scale
    )
    return jnp.where(row_mask(segment, length)[None], scores, -1e30)


def pack_grads(items, groups):
    packed = jnp.concatenate([item.reshape(-1) for item in items])
    extra = -packed.shape[0] % groups
    return jnp.pad(packed, (0, extra))


def unpack_grads(packed, items):
    result = []
    offset = 0
    for item in items:
        result.append(packed[offset : offset + item.size].reshape(item.shape))
        offset = offset + item.size
    return tuple(result)


def body(
    hidden,
    segment_ids,
    lengths,
    norm1_gain,
    norm1_shift,
    qkv_weight,
    qv_bias,
    out_weight,
    out_bias,
    norm2_gain,
    norm2_shift,
    up_weight,
    up_bias,
    down_weight,
    down_bias,
    cotangent,
):
    rows_here = hidden.shape[0]
    seq_total = segment_ids.shape[1]
    local_width = qkv_weight.shape[2]
    head_size = HEAD
    heads_here = local_width // head_size
    scale = head_size ** (-0.5)
    groups = lax.axis_size("dp")
    resid = hidden.astype(jnp.float32)
    normed1 = norm_rows(resid, norm1_gain, norm1_shift)
    normed_full = lax.all_gather(normed1.astype(jnp.bfloat16), "tensor", axis=1, tiled=True)
    project = jnp.einsum(
        "rtd,cde->crte", normed_full, qkv_weight, preferred_element_type=jnp.float32
    )
    query = (
        (project[0] + qv_bias[0])
        .astype(jnp.bfloat16)
        .reshape(rows_here, seq_total, heads_here, head_size)
    )
    keys = project[1].astype(jnp.bfloat16).reshape(rows_here, seq_total, heads_here, head_size)
    values = (
        (project[2] + qv_bias[1])
        .astype(jnp.bfloat16)
        .reshape(rows_here, seq_total, heads_here, head_size)
    )

    def forward_row(pieces):
        query_row, key_row, value_row, segment, length = pieces
        scores = masked_scores(query_row, key_row, segment, length, scale)
        top = jnp.max(scores, axis=-1, keepdims=True)
        total = jnp.sum(jnp.exp(scores - top), axis=-1, keepdims=True)
        logsum = top + jnp.log(total)
        probs = jnp.exp(scores - logsum).astype(jnp.bfloat16)
        mixed = jnp.einsum("hqk,khe->qhe", probs, value_row, preferred_element_type=jnp.float32)
        return (mixed.astype(jnp.bfloat16), logsum)

    attended, logsums = lax.map(forward_row, (query, keys, values, segment_ids, lengths))
    attended_flat = attended.reshape(rows_here, seq_total, local_width)
    branch = jnp.einsum(
        "rte,ed->rtd", attended_flat, out_weight, preferred_element_type=jnp.float32
    )
    mid = resid + lax.psum_scatter(branch, "tensor", scatter_dimension=1, tiled=True) + out_bias
    normed2 = norm_rows(mid, norm2_gain, norm2_shift)
    normed2_full = lax.all_gather(normed2.astype(jnp.bfloat16), "tensor", axis=1, tiled=True)
    inner = (
        jnp.einsum("rtd,df->rtf", normed2_full, up_weight, preferred_element_type=jnp.float32)
        + up_bias
    )
    active = jax.nn.gelu(inner).astype(jnp.bfloat16)
    branch2 = jnp.einsum("rtf,fd->rtd", active, down_weight, preferred_element_type=jnp.float32)
    output = (
        mid
        + lax.psum_scatter(
            branch2.astype(jnp.bfloat16), "tensor", scatter_dimension=1, tiled=True
        ).astype(jnp.float32)
        + down_bias
    ).astype(jnp.bfloat16)
    grad_out = cotangent.astype(jnp.float32)
    grad_full = lax.all_gather(cotangent, "tensor", axis=1, tiled=True)
    down_weight_grad = jnp.einsum(
        "rtf,rtd->fd", active, grad_full, preferred_element_type=jnp.float32
    )
    down_bias_grad = jnp.sum(grad_out, axis=(0, 1))
    grad_active = jnp.einsum(
        "rtd,fd->rtf", grad_full, down_weight, preferred_element_type=jnp.float32
    )
    gelu_back = jax.vjp(jax.nn.gelu, inner)[1]
    grad_inner = gelu_back(grad_active)[0].astype(jnp.bfloat16)
    up_weight_grad = jnp.einsum(
        "rtd,rtf->df", normed2_full, grad_inner, preferred_element_type=jnp.float32
    )
    up_bias_grad = jnp.sum(grad_inner, axis=(0, 1), dtype=jnp.float32)
    grad_normed2_part = jnp.einsum(
        "rtf,df->rtd", grad_inner, up_weight, preferred_element_type=jnp.float32
    )
    grad_normed2 = lax.psum_scatter(grad_normed2_part, "tensor", scatter_dimension=1, tiled=True)
    norm2_back = jax.vjp(norm_rows, mid, norm2_gain, norm2_shift)[1]
    grad_mid_norm, norm2_gain_grad, norm2_shift_grad = norm2_back(grad_normed2)
    grad_mid = grad_out + grad_mid_norm
    out_bias_grad = jnp.sum(grad_mid, axis=(0, 1))
    grad_mid_full = lax.all_gather(grad_mid.astype(jnp.bfloat16), "tensor", axis=1, tiled=True)
    out_weight_grad = jnp.einsum(
        "rte,rtd->ed", attended_flat, grad_mid_full, preferred_element_type=jnp.float32
    )
    grad_attended = jnp.einsum(
        "rtd,ed->rte", grad_mid_full, out_weight, preferred_element_type=jnp.float32
    )
    grad_attended = grad_attended.astype(jnp.bfloat16).reshape(
        rows_here, seq_total, heads_here, head_size
    )

    def backward_row(pieces):
        query_row, key_row, value_row, segment, length, logsum, grad_row = pieces
        scores = masked_scores(query_row, key_row, segment, length, scale)
        probs = jnp.exp(scores - logsum)
        probs_low = probs.astype(jnp.bfloat16)
        grad_values = jnp.einsum(
            "hqk,qhe->khe", probs_low, grad_row, preferred_element_type=jnp.float32
        )
        grad_probs = jnp.einsum(
            "qhe,khe->hqk", grad_row, value_row, preferred_element_type=jnp.float32
        )
        inner_sum = jnp.sum(probs * grad_probs, axis=-1, keepdims=True)
        grad_scores = (probs * (grad_probs - inner_sum)).astype(jnp.bfloat16)
        grad_query = (
            jnp.einsum("hqk,khe->qhe", grad_scores, key_row, preferred_element_type=jnp.float32)
            * scale
        )
        grad_keys = (
            jnp.einsum("hqk,qhe->khe", grad_scores, query_row, preferred_element_type=jnp.float32)
            * scale
        )
        return (
            grad_query.astype(jnp.bfloat16),
            grad_keys.astype(jnp.bfloat16),
            grad_values.astype(jnp.bfloat16),
        )

    grad_query, grad_keys, grad_values = lax.map(
        backward_row, (query, keys, values, segment_ids, lengths, logsums, grad_attended)
    )
    grad_project = jnp.stack([grad_query, grad_keys, grad_values]).reshape(
        3, rows_here, seq_total, local_width
    )
    qkv_weight_grad = jnp.einsum(
        "rtd,crte->cde", normed_full, grad_project, preferred_element_type=jnp.float32
    )
    qv_bias_grad = jnp.stack(
        [
            jnp.sum(grad_project[0], axis=(0, 1), dtype=jnp.float32),
            jnp.sum(grad_project[2], axis=(0, 1), dtype=jnp.float32),
        ]
    )
    grad_normed1_part = jnp.einsum(
        "crte,cde->rtd", grad_project, qkv_weight, preferred_element_type=jnp.float32
    )
    grad_normed1 = lax.psum_scatter(grad_normed1_part, "tensor", scatter_dimension=1, tiled=True)
    norm1_back = jax.vjp(norm_rows, resid, norm1_gain, norm1_shift)[1]
    grad_in_norm, norm1_gain_grad, norm1_shift_grad = norm1_back(grad_normed1)
    input_grad = (grad_mid + grad_in_norm).astype(jnp.bfloat16)
    all_items = (
        qkv_weight_grad,
        qv_bias_grad,
        out_weight_grad,
        up_weight_grad,
        up_bias_grad,
        down_weight_grad,
    )
    all_share = lax.psum_scatter(
        pack_grads(all_items, groups), "dp", scatter_dimension=0, tiled=True
    )
    all_whole = lax.all_gather(all_share.astype(jnp.bfloat16), "dp", axis=0, tiled=True).astype(
        all_share.dtype
    )
    (
        qkv_weight_grad,
        qv_bias_grad,
        out_weight_grad,
        up_weight_grad,
        up_bias_grad,
        down_weight_grad,
    ) = unpack_grads(all_whole, all_items)
    (
        norm1_gain_grad,
        norm1_shift_grad,
        out_bias_grad,
        norm2_gain_grad,
        norm2_shift_grad,
        down_bias_grad,
    ) = lax.psum(
        (
            norm1_gain_grad,
            norm1_shift_grad,
            out_bias_grad,
            norm2_gain_grad,
            norm2_shift_grad,
            down_bias_grad,
        ),
        ("dp", "tensor"),
    )
    return (
        output,
        input_grad,
        norm1_gain_grad,
        norm1_shift_grad,
        qkv_weight_grad,
        qv_bias_grad,
        out_weight_grad,
        out_bias_grad,
        norm2_gain_grad,
        norm2_shift_grad,
        up_weight_grad,
        up_bias_grad,
        down_weight_grad,
        down_bias_grad,
    )


def solution(mesh):
    in_specs = (
        P("dp", "tensor", None),
        P("dp", None),
        P("dp"),
        P(),
        P(),
        P(None, None, "tensor"),
        P(None, "tensor"),
        P("tensor", None),
        P(),
        P(),
        P(),
        P(None, "tensor"),
        P("tensor"),
        P("tensor", None),
        P(),
        P("dp", "tensor", None),
    )
    out_specs = (
        P("dp", "tensor", None),
        P("dp", "tensor", None),
        P(),
        P(),
        P(None, None, "tensor"),
        P(None, "tensor"),
        P("tensor", None),
        P(),
        P(),
        P(),
        P(None, "tensor"),
        P("tensor"),
        P("tensor", None),
        P(),
    )
    return jax.shard_map(body, mesh=mesh, in_specs=in_specs, out_specs=out_specs, check_vma=False)
```

profile of v0, /device:TPU:1, one launch (start us, length us, event | category | flops | bytes accessed | tf_op | source)
XLA Modules:
  0.0 1774.1 jit_solution(7684851957845038675)
XLA Ops:
  7.3 1.5 convert_reduce_fusion.1
  8.7 1.5 fusion.51
  11.4 2.3 fusion.49
  14.7 4.1 fusion.2
  18.8 57.2 %all-gather.5.cloned.1.call-done = bf16[1,1280,1120]{2,1,0:T(8,128)(2,1)} async-done(((bf16[1,320,1120]{2,1,0:T(8,128)(2,1)}), bf16[1,1280,1120]{2,1,0:T(8,128)(2,1)}) %all-gather.5.cloned.1.call-update) | async-done | bytes 2867216 | tf_op jit(solution)/shard_map/all_gather | solution.py:75
  76.0 5.4 convolution_bitcast_fusion.3
  83.4 13.7 fusion.70
  97.1 13.2 exponential_reduce_fusion
  110.4 15.9 fusion.36
  126.3 5.5 convolution_bitcast_fusion.2
  131.8 12.9 copy.56
  146.7 207.1 %all-reduce.14.cloned.1.call-done = f32[1,1280,1120]{2,0,1:T(1,128)} async-done(((f32[1,1280,1120]{2,0,1:T(1,128)}), f32[1,1280,1120]{2,0,1:T(1,128)}) %all-reduce.14.cloned.1.call-update) | async-done | bytes 5734416
  353.8 2.4 constant_dynamic-slice_fusion.2
  359.7 58.4 %all-gather.7.cloned.1.call-done = bf16[1,1280,1120]{2,1,0:T(8,128)(2,1)} async-done(((bf16[1,320,1120]{2,1,0:T(8,128)(2,1)}), bf16[1,1280,1120]{2,1,0:T(8,128)(2,1)}) %all-gather.7.cloned.1.call-update) | async-done | bytes 2867216 | tf_op jit(solution)/shard_map/all_gather | solution.py:108
  418.1 9.0 convolution_add_fusion
  427.1 51.3 %all-gather.9.cloned.1.call-done = bf16[1,1280,1120]{2,1,0:T(8,128)(2,1)} async-done(((bf16[1,320,1120]{2,1,0:T(8,128)(2,1)}), bf16[1,1280,1120]{2,1,0:T(8,128)(2,1)}) %all-gather.9.cloned.1.call-update) | async-done | bytes 2867216 | tf_op jit(solution)/shard_map/all_gather | solution.py:123
  478.4 9.3 convert_reduce_fusion
  487.7 1.6 copy-done.47
  489.3 5.7 convolution_bitcast_fusion
  495.0 12.9 copy.59
  508.5 8.4 fusion.4
  516.9 12.8 copy.77
  529.7 4.7 copy.102
  534.5 182.4 %all-reduce.16.cloned.1.call-done = f32[1,1280,1120]{2,0,1:T(1,128)} async-done(((f32[1,1280,1120]{2,0,1:T(1,128)}), f32[1,1280,1120]{2,0,1:T(1,128)}) %all-reduce.16.cloned.1.call-update) | async-done | bytes 5734416
  716.9 3.8 fusion.62
  722.9 52.8 %reduce-scatter.4.cloned.1.call-done = bf16[320,1120]{1,0:T(8,128)(2,1)} async-done(((bf16[1280,1120]{1,0:T(8,128)(2,1)}), bf16[320,1120]{1,0:T(8,128)(2,1)}) %reduce-scatter.4.cloned.1.call-update) | async-done | bytes 716816
  775.7 2.0 reshape_bitcast_fusion
  777.7 1.4 fusion.64
  783.6 9.1 fusion.28
  792.6 7.1 reshape.473
  799.7 10.8 fusion.22
  810.5 7.2 reshape.474
  817.7 24.1 %all-gather.11.cloned.1.call-done = bf16[1,1280,1120]{2,1,0:T(8,128)(2,1)} async-done(((bf16[1,320,1120]{2,1,0:T(8,128)(2,1)}), bf16[1,1280,1120]{2,1,0:T(8,128)(2,1)}) %all-gather.11.cloned.1.call-update) | async-done | bytes 2867216 | tf_op jit(solution)/shard_map/all_gather | solution.py:145
  841.8 3.0 fusion.33
  844.8 21.7 %multiply_reduce_fusion = (f32[5,1280]{1,0:T(8,128)S(1)}, f32[5,1280,1280]{1,2,0:T(8,128)}) fusion(f32[5,1280,1280]{1,2,0:T(8,128)} %get-tuple-element.144, f32[5,1280]{1,0:T(8,128)S(1)} %log_add_fusion, bf16[1280,5,56]{0,2,1:T(8,128)(2,1)S(1)} %bitcast.112, f32[1280,5,56]{0,2,1:T(8,128)S(1)} %bitcast.108, f32[5,56]{1,0:T(8,128)S(1)} %add.152), kind=kOutput, calls=%fused_computation.3 | convolution fusion | flops 942790400 | bytes 67738720 | tf_op jit(solution)/shard_map/while/body/eval_jaxpr/qhe,khe->hqk/dot_general | solution.py:164
  866.5 14.7 convert_reduce_fusion.3
  881.2 27.5 %multiply_convert_fusion = bf16[5,1280,1280]{1,2,0:T(8,128)(2,1)} fusion(f32[5,1280,1280]{1,2,0:T(8,128)} %get-tuple-element.146, f32[5,1280,1280]{1,2,0:T(8,128)} %get-tuple-element.144, f32[5,1280]{1,0:T(8,128)S(1)} %get-tuple-element.145, f32[5,1280]{1,0:T(8,128)S(1)} %log_add_fusion), kind=kLoop, calls=%fused_computation.2 | loop fusion | flops 32768000 | bytes 81971200 | tf_op jit(solution)/shard_map/while/body/eval_jaxpr/convert_element_type | solution.py:168
  908.7 9.5 convert_reduce_fusion.4
  918.2 10.8 fusion.32
  929.2 6.9 convolution_bitcast_fusion.4
  936.1 5.8 copy.70
  941.9 7.6 reshape.470
  949.5 2.9 fusion.18
  953.4 122.8 %concatenate.4 = f32[3764880]{0:T(1024)} concatenate(f32[940800]{0:T(1024)} %reshape.470, f32[560]{0:T(1024)S(1)} %reshape.471, f32[313600]{0:T(1024)S(1)} %reshape.472, f32[1254400]{0:T(1024)} %reshape.473, f32[1120]{0:T(1024)S(1)} %get-tuple-element.151, f32[1254400]{0:T(1024)} %reshape.474), dimensions={0} | concatenate | bytes 30119040 | tf_op jit(solution)/shard_map/concatenate | solution.py:34
  1076.2 296.5 %all-reduce.19 = bf16[3764880]{0:T(1024)(128)(2,1)} all-reduce(f32[3764880]{0:T(1024)} %concatenate.4), channel_id=6, replica_groups=mesh['dp'=8,'tensor'=4] {'dp'}, use_global_device_ids=true, to_apply=%region_22.23.clone | all-reduce | flops 3764880 | bytes 22589280
  1372.7 1.7 dynamic-slice.14
  1374.4 3.5 broadcast.224
  1377.9 14.9 dynamic-update-slice
  1394.2 7.2 convolution_bitcast_fusion.1
  1401.4 13.2 copy.67
  1414.6 93.8 %all-reduce.12.cloned.1.call-done = bf16[3764880]{0:T(1024)(128)(2,1)} async-done(((bf16[3764880]{0:T(1024)(128)(2,1)}), bf16[3764880]{0:T(1024)(128)(2,1)}) %all-reduce.12.cloned.1.call-update) | async-done | bytes 7529776
  1508.4 6.8 fusion.67
  1515.3 7.1 reshape.477
  1522.4 6.9 reshape.478
  1529.2 3.6 slice.63
  1532.9 7.2 reshape.475
  1540.0 5.9 copy.72
  1546.0 1.4 slice.65
  1547.4 1.8 reshape.476
  1550.6 1.4 slice.67
  1551.9 169.3 %all-reduce.18.cloned.1.call-done = f32[1,1280,1120]{2,0,1:T(1,128)} async-done(((f32[1,1280,1120]{2,0,1:T(1,128)}), f32[1,1280,1120]{2,0,1:T(1,128)}) %all-reduce.18.cloned.1.call-update) | async-done | bytes 5734416
  1721.2 3.2 fusion.63
  1726.0 1.7 convert_reduce_fusion.2
  1727.7 39.7 %all-reduce.5 = (f32[1120]{0:T(1024)}, f32[1120]{0:T(1024)}, f32[1120]{0:T(1024)}, f32[1120]{0:T(1024)}, f32[1120]{0:T(1024)}, /*index=5*/f32[1120]{0:T(1024)}) all-reduce(f32[1120]{0:T(1024)S(1)} %get-tuple-element.115, f32[1120]{0:T(1024)S(1)} %get-tuple-element.129, ...), channel_id=1, replica_groups=mesh['dp'=8,'tensor'=4] {'dp','tensor'}, use_global_device_ids=true, to_apply=%region_16.17 | all-reduce | flops 6720 | bytes 53760 | tf_op jit(solution)/shard_map/psum | solution.py:234
  (145 shorter events, 19.3 us)
Async XLA Ops:
  7.2 471.2 %copy-start = (bf16[1120,1120]{1,0:T(8,128)(2,1)S(1)}, bf16[1120,1120]{1,0:T(8,128)(2,1)}, u32[]{:S(2)}) copy-start(bf16[1120,1120]{1,0:T(8,128)(2,1)} %param.29) | copy-start | bytes 7526404
  7.2 6.6 copy-start.41
  7.2 7.5 copy-start.40
  7.2 68.8 %all-gather.5.cloned.1.call-start = ((), (), s32[]{:S(2)}) async-start(), calls=%async_computation.1 | async-start | bytes 3686400 | tf_op jit(solution)/shard_map/all_gather | solution.py:75
  8.7 2.1 copy-start.27
  10.2 0.6 copy-start.35
  10.8 0.6 copy-start.31
  13.8 340.0 %all-reduce.14.cloned.1.call-start = ((), (), s32[]{:S(2)}) async-start(), calls=%async_computation.7 | async-start | bytes 11796480
  13.9 68.9 %copy-start.23 = (f32[5,56]{1,0:T(8,128)}, f32[5,56]{1,0:T(8,128)S(1)}, u32[]{:S(2)}) copy-start(f32[5,56]{1,0:T(8,128)S(1)} %add.155) | copy-start | bytes 3364
  81.4 2.0 copy-start.6
  82.7 14.4 copy-start.7
  82.8 14.3 copy-start.14
  126.3 5.5 copy-start.18
  144.8 0.7 copy-start.46
  144.8 211.3 %copy-start.4 = (bf16[1,320,1120]{2,1,0:T(8,128)(2,1)S(1)}, bf16[1,320,1120]{2,1,0:T(8,128)(2,1)}, u32[]{:S(2)}) copy-start(bf16[1,320,1120]{2,1,0:T(8,128)(2,1)} %param.16) | copy-start | bytes 2150404
  144.8 211.3 %copy-start.37 = (f32[1120]{0:T(1024)S(1)}, f32[1120]{0:T(1024)}, u32[]{:S(2)}) copy-start(f32[1120]{0:T(1024)} %param.24) | copy-start | bytes 13444
  144.8 273.3 %all-gather.7.cloned.1.call-start = ((), (), s32[]{:S(2)}) async-start(), calls=%async_computation.2 | async-start | bytes 3686400 | tf_op jit(solution)/shard_map/all_gather | solution.py:108
  356.2 1.4 copy-start.26
  356.2 1.4 copy-start.38
  356.5 1.1 copy-start.2
  356.5 61.6 %copy-start.45 = (f32[1120]{0:T(1024)S(1)}, f32[1120]{0:T(1024)}, u32[]{:S(2)}) copy-start(f32[1120]{0:T(1024)} %param.28) | copy-start | bytes 13444
  358.8 119.6 %all-gather.9.cloned.1.call-start = ((), (), s32[]{:S(2)}) async-start(), calls=%async_computation.3 | async-start | bytes 3686400 | tf_op jit(solution)/shard_map/all_gather | solution.py:123
  359.4 357.5 %all-reduce.16.cloned.1.call-start = ((), (), s32[]{:S(2)}) async-start(), calls=%async_computation.8 | async-start | bytes 11796480
  478.4 10.8 copy-start.43
  487.7 1.6 copy-start.47
  508.0 267.7 %reduce-scatter.4.cloned.1.call-start = ((), (), s32[]{:S(2)}) async-start(), calls=%async_computation.6 | async-start | bytes 3686400
  534.4 187.4 %copy-start.3 = (f32[1,320,1120]{2,1,0:T(8,128)S(1)}, f32[1,320,1120]{2,1,0:T(8,128)}, u32[]{:S(2)}) copy-start(f32[1,320,1120]{2,1,0:T(8,128)} %copy-done.2) | copy-start | bytes 4300804
  534.5 307.3 %all-gather.11.cloned.1.call-start = ((), (), s32[]{:S(2)}) async-start(), calls=%async_computation.4 | async-start | bytes 3686400 | tf_op jit(solution)/shard_map/all_gather | solution.py:145
  720.7 1.1 copy-start.11
  720.7 57.0 %copy-start.39 = (f32[1120]{0:T(1024)S(1)}, f32[1120]{0:T(1024)}, u32[]{:S(2)}) copy-start(f32[1120]{0:T(1024)} %param.30) | copy-start | bytes 13444
  775.7 2.0 copy-start.12
  777.7 2.6 copy-start.16
  779.2 1.1 copy-start.9
  779.2 2.5 copy-start.42
  779.2 13.4 copy-start.33
  781.4 727.0 %all-reduce.12.cloned.1.call-start = ((), (), s32[]{:S(2)}) async-start(), calls=%async_computation.5 | async-start | bytes 15060992
  810.5 31.3 %copy-start.44 = (bf16[280,1120]{1,0:T(8,128)(2,1)S(1)}, bf16[280,1120]{1,0:T(8,128)(2,1)}, u32[]{:S(2)}) copy-start(bf16[280,1120]{1,0:T(8,128)(2,1)} %param.23) | copy-start | bytes 1881604
  817.7 27.1 %copy-start.13 = (f32[1,1,1280,280]{2,3,0,1:T(8,128)S(1)}, f32[1,1,1280,280]{2,3,0,1:T(8,128)}, u32[]{:S(2)}) copy-start(f32[1,1,1280,280]{2,3,0,1:T(8,128)} %get-tuple-element.137) | copy-start | bytes 4300804
  881.2 27.5 %copy-start.15 = (bf16[1,1,1280,280]{2,3,0,1:T(8,128)(2,1)S(1)}, bf16[1,1,1280,280]{2,3,0,1:T(8,128)(2,1)}, u32[]{:S(2)}) copy-start(bf16[1,1,1280,280]{2,3,0,1:T(8,128)(2,1)} %copy-done.14) | copy-start | bytes 2150404
  908.6 9.5 copy-start.8
  908.6 9.5 copy-start.24
  918.2 11.0 copy-start.20
  941.9 7.6 copy-start.19
  1392.8 1.1 copy-start.21
  1392.8 1.3 copy-start.22
  1392.9 328.4 %all-reduce.18.cloned.1.call-start = ((), (), s32[]{:S(2)}) async-start(), calls=%async_computation.9 | async-start | bytes 11796480
  1547.4 177.0 %copy-start.5 = (bf16[1,320,1120]{2,1,0:T(8,128)(2,1)S(1)}, bf16[1,320,1120]{2,1,0:T(8,128)(2,1)}, u32[]{:S(2)}) copy-start(bf16[1,320,1120]{2,1,0:T(8,128)(2,1)} %param.16) | copy-start | bytes 2150404
  1547.4 177.0 %copy-start.25 = (f32[1120]{0:T(1024)S(1)}, f32[1120]{0:T(1024)}, u32[]{:S(2)}) copy-start(f32[1120]{0:T(1024)} %param.19) | copy-start | bytes 13444
  1547.4 177.0 %copy-start.28 = (f32[320]{0:T(512)S(1)}, f32[320]{0:T(512)}, u32[]{:S(2)}) copy-start(f32[320]{0:T(512)} %copy-done.27) | copy-start | bytes 3844
  1549.2 175.7 %copy-start.36 = (f32[320]{0:T(512)S(1)}, f32[320]{0:T(512)}, u32[]{:S(2)}) copy-start(f32[320]{0:T(512)} %copy-done.35) | copy-start | bytes 3844
  1549.2 175.7 %copy-start.32 = (f32[320]{0:T(512)S(1)}, f32[320]{0:T(512)}, u32[]{:S(2)}) copy-start(f32[320]{0:T(512)} %copy-done.31) | copy-start | bytes 3844
  1724.4 1.4 copy-start.10
  1724.4 1.6 copy-start.17
  1724.4 1.5 copy-start.34
  1724.9 42.5 %copy-start.1 = (bf16[1120,1120]{1,0:T(8,128)(2,1)S(1)}, bf16[1120,1120]{1,0:T(8,128)(2,1)}, u32[]{:S(2)}) copy-start(bf16[1120,1120]{1,0:T(8,128)(2,1)} %param.29) | copy-start | bytes 7526404
  1725.6 2.1 copy-start.29
  1725.6 2.1 copy-start.30
Sparse Core Ops, SparseCore 0:
  13.9 62.0 all-gather.4
  144.9 208.7 all-reduce.13
  358.9 59.0 all-gather.6
  419.5 58.8 all-gather.8
  508.1 208.7 all-reduce.15
  719.6 56.0 reduce-scatter.3
  781.5 60.1 all-gather.10
  1393.0 115.4 all-reduce.11
  1510.8 210.3 all-reduce.17
where the time goes:
time: 1790 us; the launch traced here: 1770 us
  waiting for transfers between devices  897 us (50%)
  blocking collectives  336 us (19%)
  local copies, waits for them, and re-layouts  287 us (16%)
  matrix products  170 us (9%)
  other arithmetic  65.4 us (4%)
    unnamed x14, waiting for transfers between devices  706 us
    unnamed x1, blocking collectives  297 us
    concatenate x1, local copies, waits for them, and re-layouts, pack_grads(): packed = jnp.concatenate([item.reshape(-1) for item in items])  123 us
    all_gather x1, waiting for transfers between devices, body(): lax.all_gather(normed2.astype(jnp.bfloat16), 'tensor', axis=1, tiled=True)  58.4 us
    unnamed x106, local copies, waits for them, and re-layouts  57.7 us
    all_gather x1, waiting for transfers between devices, body(): lax.all_gather(normed1.astype(jnp.bfloat16), 'tensor', axis=1, tiled=True)  57.2 us
    all_gather x1, waiting for transfers between devices, body(): grad_full = lax.all_gather(cotangent, 'tensor', axis=1, tiled=True)  51.3 us
    psum x1, blocking collectives, body(): lax.psum((norm1_gain_grad, norm1_shift_grad, out_bias_grad, norm2_gain_gr...  39.7 us
  transfers between devices with their start and end apart: 9, of which 9 were waited for; matrix products, arithmetic and copies ran while one was open for 8% of the time, Pallas kernels for 0%

commit v1 on v0

v1 whole, which is shorter than its diff:
```python
import functools
import math

import jax
import jax.numpy as jnp
from jax import lax
from jax.experimental import pallas as pl
from jax.experimental.pallas import tpu as pltpu
from jax.sharding import PartitionSpec as P

HEAD = 56
EPS = 1e-05
LANES = 128
BLK = 256
BF = jnp.bfloat16
F32 = jnp.float32


def head_window(h):
    lo, hi = h * HEAD, (h + 1) * HEAD
    first = lo // LANES * LANES
    last = -(-hi // LANES) * LANES
    return first, last


def head_mask(h, rows):
    first, last = head_window(h)
    lane = lax.broadcasted_iota(jnp.int32, (rows, last - first), 1) + first
    return (lane >= h * HEAD) & (lane < (h + 1) * HEAD)


def stage_in(rank, src, dst, shard, width):
    wide = dst.shape[1]
    for s in range(src.shape[0] // shard):
        rel = pl.multiple_of((rank ^ s) * shard, 16)
        dst[s * shard : (s + 1) * shard, :width] = src[pl.ds(rel, shard), :]
    if wide > width:
        dst[:, width:] = jnp.zeros((dst.shape[0], wide - width), dst.dtype)


def stage_out(rank, src, dst, shard, width):
    for s in range(dst.shape[0] // shard):
        rel = pl.multiple_of((rank ^ s) * shard, 16)
        dst[pl.ds(rel, shard), :] = src[s * shard : (s + 1) * shard, :width]


def tile_mask(start_row, qb, kb):
    kpos = kb * BLK + lax.broadcasted_iota(jnp.int32, (BLK, BLK), 0)
    qpos = qb * BLK + lax.broadcasted_iota(jnp.int32, (BLK, BLK), 1)
    return (kpos <= qpos) & (kpos >= start_row)


def dot_nt(a, b):
    return lax.dot_general(a, b, (((1,), (1,)), ((), ())), preferred_element_type=F32)


def attn_fwd_kernel(heads, shard, meta, start, q, k, v, out, lse, qs, ks, vs, vt, os, ot, ms, ls, acc):
    seq, width = q.shape
    scale2 = HEAD ** (-0.5) * math.log2(math.e)
    rank = meta[0]
    stage_in(rank, q, qs, shard, width)
    stage_in(rank, k, ks, shard, width)
    stage_in(rank, v, vs, shard, width)
    blocks = seq // BLK

    @pl.loop(0, blocks)
    def _(b):
        rows = pl.ds(pl.multiple_of(b * BLK, BLK), BLK)
        flipped = vs[rows, :].astype(F32).T
        for h in range(heads):
            vt[h, :, rows] = flipped[h * HEAD : (h + 1) * HEAD, :].astype(BF)

    lse[...] = jnp.zeros_like(lse)

    @pl.loop(0, blocks)
    def _(b):
        rows = pl.ds(pl.multiple_of(b * BLK, BLK), BLK)
        start_row = start[:, rows]
        ms[...] = jnp.full_like(ms, -1e30)
        ls[...] = jnp.zeros_like(ls)
        acc[...] = jnp.zeros_like(acc)

        def tile(kb, carry):
            krows = pl.ds(pl.multiple_of(kb * BLK, BLK), BLK)
            mask = tile_mask(start_row, b, kb)
            for h in range(heads):
                first, last = head_window(h)
                qm = jnp.where(head_mask(h, BLK), qs[rows, first:last], 0)
                s = dot_nt(ks[krows, first:last], qm) * scale2
                s = jnp.where(mask, s, -1e30)
                old = ms[h : h + 1, :]
                new = jnp.maximum(old, jnp.max(s, axis=0, keepdims=True))
                p = jnp.exp2(s - new)
                p = jnp.where(mask, p, 0.0)
                fade = jnp.exp2(old - new)
                ms[h : h + 1, :] = new
                ls[h : h + 1, :] = ls[h : h + 1, :] * fade + jnp.sum(p, axis=0, keepdims=True)
                acc[h] = acc[h] * fade + jnp.dot(
                    vt[h, :, krows], p.astype(BF), preferred_element_type=F32
                )
            return carry

        lax.fori_loop(meta[1 + b], b + 1, tile, 0)
        for h in range(heads):
            total = ls[h : h + 1, :]
            lse[h : h + 1, rows] = ms[h : h + 1, :] + jnp.log(total) * math.log2(math.e)
            ot[h * HEAD : (h + 1) * HEAD, :] = acc[h] / total
        os[rows, :] = ot[...].T.astype(BF)

    stage_out(rank, os, out, shard, width)


def attn_bwd_kernel(
    heads, shard, meta, start, q, k, v, o, do, lse, dq, dk, dv,
    qs, ks, vs, dos, kt, delta, dqs, dks, dvs, dqt, qm, dm,
):
    seq, width = q.shape
    scale = HEAD ** (-0.5)
    scale2 = scale * math.log2(math.e)
    rank = meta[0]
    blocks = seq // BLK
    stage_in(rank, o, vs, shard, width)
    stage_in(rank, do, dos, shard, width)

    @pl.loop(0, blocks)
    def _(b):
        rows = pl.ds(pl.multiple_of(b * BLK, BLK), BLK)
        flipped = (vs[rows, :].astype(F32) * dos[rows, :].astype(F32)).T
        for h in range(heads):
            delta[h : h + 1, rows] = jnp.sum(
                flipped[h * HEAD : (h + 1) * HEAD, :], axis=0, keepdims=True
            )

    stage_in(rank, q, qs, shard, width)
    stage_in(rank, k, ks, shard, width)
    stage_in(rank, v, vs, shard, width)

    @pl.loop(0, blocks)
    def _(b):
        rows = pl.ds(pl.multiple_of(b * BLK, BLK), BLK)
        flipped = ks[rows, :].astype(F32).T
        for h in range(heads):
            kt[h, :, rows] = flipped[h * HEAD : (h + 1) * HEAD, :].astype(BF)

    dks[...] = jnp.zeros_like(dks)
    dvs[...] = jnp.zeros_like(dvs)
    dqt[...] = jnp.zeros_like(dqt)

    @pl.loop(0, blocks)
    def _(b):
        rows = pl.ds(pl.multiple_of(b * BLK, BLK), BLK)
        start_row = start[:, rows]
        dqt[...] = jnp.zeros_like(dqt)
        for h in range(heads):
            first, last = head_window(h)
            keep = head_mask(h, BLK)
            qm[h, :, : last - first] = jnp.where(keep, qs[rows, first:last], 0)
            dm[h, :, : last - first] = jnp.where(keep, dos[rows, first:last], 0)

        def tile(kb, carry):
            krows = pl.ds(pl.multiple_of(kb * BLK, BLK), BLK)
            mask = tile_mask(start_row, b, kb)
            for h in range(heads):
                first, last = head_window(h)
                qh = qm[h, :, : last - first]
                dh = dm[h, :, : last - first]
                s = dot_nt(ks[krows, first:last], qh) * scale2
                p = jnp.where(mask, jnp.exp2(s - lse[h : h + 1, rows]), 0.0)
                dp = dot_nt(vs[krows, first:last], dh)
                ds = (p * (dp - delta[h : h + 1, rows])).astype(BF)
                dvs[krows, first:last] += jnp.dot(p.astype(BF), dh, preferred_element_type=F32)
                dks[krows, first:last] += jnp.dot(ds, qh, preferred_element_type=F32)
                dqt[h * HEAD : (h + 1) * HEAD, :] += jnp.dot(
                    kt[h, :, krows], ds, preferred_element_type=F32
                )
            return carry

        lax.fori_loop(meta[1 + b], b + 1, tile, 0)
        dqs[rows, :] = (dqt[...].T * scale).astype(BF)

    stage_out(rank, dqs, dq, shard, width)
    for s in range(seq // shard):
        rel = pl.multiple_of((rank ^ s) * shard, 16)
        here = slice(s * shard, (s + 1) * shard)
        dk[pl.ds(rel, shard), :] = (dks[here, :width] * scale).astype(BF)
        dv[pl.ds(rel, shard), :] = dvs[here, :width].astype(BF)


def vmem():
    return pl.BlockSpec(memory_space=pltpu.VMEM)


def smem():
    return pl.BlockSpec(memory_space=pltpu.SMEM)


def attn_cost(seq, width, products):
    return pl.CostEstimate(
        flops=products * seq * seq * width,
        bytes_accessed=8 * seq * width * 2,
        transcendentals=seq * seq * width // (2 * HEAD),
    )


def attn_fwd(meta, start, q, k, v, shard):
    seq, width = q.shape
    heads = width // HEAD
    wide = -(-width // LANES) * LANES
    return pl.pallas_call(
        functools.partial(attn_fwd_kernel, heads, shard),
        out_shape=(
            jax.ShapeDtypeStruct((seq, width), BF),
            jax.ShapeDtypeStruct((8, seq), F32),
        ),
        in_specs=[smem()] + [vmem()] * 4,
        out_specs=(vmem(), vmem()),
        scratch_shapes=[
            pltpu.VMEM((seq, wide), BF),
            pltpu.VMEM((seq, wide), BF),
            pltpu.VMEM((seq, wide), BF),
            pltpu.VMEM((heads, HEAD, seq), BF),
            pltpu.VMEM((seq, wide), BF),
            pltpu.VMEM((wide, BLK), F32),
            pltpu.VMEM((8, BLK), F32),
            pltpu.VMEM((8, BLK), F32),
            pltpu.VMEM((heads, HEAD, BLK), F32),
        ],
        cost_estimate=attn_cost(seq, width, 3),
        name="attn_fwd",
    )(meta, start, q, k, v)


def attn_bwd(meta, start, q, k, v, o, do, lse, shard):
    seq, width = q.shape
    heads = width // HEAD
    wide = -(-width // LANES) * LANES
    grad = jax.ShapeDtypeStruct((seq, width), BF)
    return pl.pallas_call(
        functools.partial(attn_bwd_kernel, heads, shard),
        out_shape=(grad, grad, grad),
        in_specs=[smem()] + [vmem()] * 7,
        out_specs=(vmem(), vmem(), vmem()),
        scratch_shapes=[
            pltpu.VMEM((seq, wide), BF),
            pltpu.VMEM((seq, wide), BF),
            pltpu.VMEM((seq, wide), BF),
            pltpu.VMEM((seq, wide), BF),
            pltpu.VMEM((heads, HEAD, seq), BF),
            pltpu.VMEM((8, seq), F32),
            pltpu.VMEM((seq, wide), BF),
            pltpu.VMEM((seq, wide), F32),
            pltpu.VMEM((seq, wide), F32),
            pltpu.VMEM((wide, BLK), F32),
            pltpu.VMEM((heads, BLK, 2 * LANES), BF),
            pltpu.VMEM((heads, BLK, 2 * LANES), BF),
        ],
        cost_estimate=attn_cost(seq, width, 8),
        name="attn_bwd",
    )(meta, start, q, k, v, o, do, lse)


AXES = ("dp", "tensor")


def send(x, rule):
    nd, nt = lax.axis_size("dp"), lax.axis_size("tensor")
    pairs = []
    for d in range(nd):
        for t in range(nt):
            to = rule(d, t)
            if to is not None:
                pairs.append((d * nt + t, to[0] * nt + to[1]))
    return lax.ppermute(x, AXES, pairs)


def is_home(d, t):
    return (d & 1) == (t >> 1)


def swap_rule(d, t):
    return (d, t) if is_home(d, t) else (d ^ 1, t ^ 2)


def gather4(x):
    xz = send(x, lambda d, t: (d, t ^ 1))
    xc = send(x, lambda d, t: (d ^ 1, t))
    xzc = send(xz, lambda d, t: (d ^ 1, t))
    return jnp.concatenate([x, xz, xc, xzc], axis=0)


def scatter4(part):
    part = part.astype(BF)
    rows = part.shape[0] // 4
    other = send(part[2 * rows :], lambda d, t: (d ^ 1, t))
    far = part[rows : 2 * rows].astype(F32) + other[rows:].astype(F32)
    far = send(far.astype(BF), lambda d, t: (d, t ^ 1))
    return part[:rows].astype(F32) + other[:rows].astype(F32) + far.astype(F32)


def pad_rows(x, unit):
    extra = -x.shape[0] % unit
    return jnp.pad(x, ((0, extra), (0, 0))) if extra else x


def spread_weight(w, home, column, columns):
    rows = w.shape[0]
    w = pad_rows(w, 8 * columns)
    unit = w.shape[0] // columns

    def piece(index):
        return lax.dynamic_slice_in_dim(w, index * unit, unit, 0)

    mine = send(piece(column), lambda d, t: (d, t ^ 2) if is_home(d, t) else None)
    whole = jnp.zeros_like(w)
    for m in range(columns):
        got = mine
        if m:
            got = send(mine, lambda d, t: None if is_home(d, t) else (d ^ (2 * m), t))
        index = column ^ m
        whole = lax.dynamic_update_slice_in_dim(
            whole, jnp.where(home, piece(index), got), index * unit, 0
        )
    return whole[:rows]


def reduce_grad(g, home, column, columns):
    rows = g.shape[0]
    bits = columns.bit_length() - 1
    g = pad_rows(g, 16 * columns)
    half = g.shape[0] // 2
    done = []
    for side in range(2):
        piece = g[side * half : (side + 1) * half]
        order = [(b + side) % bits for b in range(bits)] if bits else []
        for b in order:
            n = piece.shape[0] // 2
            bit = (column >> b) & 1
            keep = lax.dynamic_slice_in_dim(piece, bit * n, n, 0)
            away = lax.dynamic_slice_in_dim(piece, (1 - bit) * n, n, 0)
            got = send(away, lambda d, t: (d ^ (2 << b), t))
            piece = (keep.astype(F32) + got.astype(F32)).astype(BF)
        got = send(piece, lambda d, t: None if is_home(d, t) else (d, t ^ 2))
        piece = (piece.astype(F32) + got.astype(F32)).astype(BF)
        for b in reversed(order):
            bit = (column >> b) & 1
            got = send(piece, lambda d, t: (d ^ (2 << b), t) if is_home(d, t) else None)
            first = jnp.where(bit == 0, piece, got)
            second = jnp.where(bit == 0, got, piece)
            piece = jnp.concatenate([first, second], axis=0)
        done.append(piece)
    whole = jnp.concatenate(done, axis=0)[:rows]
    other = send(whole, lambda d, t: (d ^ 1, t) if is_home(d, t) else None)
    return jnp.where(home, whole, other).astype(F32)


def sum_all(x):
    for axis in range(2):
        size = (lax.axis_size("dp"), lax.axis_size("tensor"))[axis]
        step = 1
        while step < size:
            x = x + send(x, lambda d, t: (d ^ step, t) if axis == 0 else (d, t ^ step))
            step *= 2
    return x


def norm_parts(values):
    center = values - jnp.mean(values, axis=-1, keepdims=True)
    rstd = lax.rsqrt(jnp.mean(center * center, axis=-1, keepdims=True) + EPS)
    return center * rstd, rstd


def norm_back(grad, hat, rstd, gain):
    gn = grad * gain
    return rstd * (
        gn
        - jnp.mean(gn, axis=-1, keepdims=True)
        - hat * jnp.mean(gn * hat, axis=-1, keepdims=True)
    )


def mm(a, b):
    return jnp.dot(a, b, preferred_element_type=F32)


def mm_nt(a, b):
    return lax.dot_general(a, b, (((1,), (1,)), ((), ())), preferred_element_type=F32)


def mm_tn(a, b):
    return lax.dot_general(a, b, (((0,), (0,)), ((), ())), preferred_element_type=F32)


def body(
    hidden,
    segment_ids,
    lengths,
    norm1_gain,
    norm1_shift,
    qkv_weight,
    qv_bias,
    out_weight,
    out_bias,
    norm2_gain,
    norm2_shift,
    up_weight,
    up_bias,
    down_weight,
    down_bias,
    cotangent,
):
    _, shard, model = hidden.shape
    seq = segment_ids.shape[1]
    width = qkv_weight.shape[2]
    hidden_units = up_weight.shape[1]
    d, t = lax.axis_index("dp"), lax.axis_index("tensor")
    columns = lax.axis_size("dp") // 2
    column = d >> 1
    home = is_home(d, t)
    rank = 2 * (d & 1) + (t & 1)

    own = send(hidden[0], swap_rule)
    full = gather4(own)
    ids = jnp.concatenate([segment_ids[0], lengths])
    ids = send(ids, swap_rule)
    length = ids[seq]
    places = jnp.arange(seq, dtype=jnp.int32)
    ids = jnp.where(places < length, ids[:seq], 16 + places)
    start = jnp.sum((ids[None, :] < ids[:, None]).astype(jnp.int32), axis=1)
    meta = jnp.concatenate([rank[None], start[::BLK] // BLK]).astype(jnp.int32)
    start = start[None, :]

    w_qkv = spread_weight(
        jnp.concatenate([qkv_weight[0], qkv_weight[1], qkv_weight[2]], axis=0), home, column, columns
    ).reshape(3, model, width)
    bias = jnp.concatenate([qv_bias.reshape(-1), up_bias])
    far_bias = send(bias, lambda d, t: (d, t ^ 2) if is_home(d, t) else None)
    bias = jnp.where(home, bias, far_bias)
    b_q, b_v, b_up = bias[:width], bias[width : 2 * width], bias[2 * width :]

    cot, own, up_w, down_w, out_w = lax.optimization_barrier(
        (cotangent[0], own, up_weight, down_weight, out_weight)
    )
    w_out = spread_weight(out_w, home, column, columns)
    w_up = spread_weight(up_w, home, column, columns)
    w_down = spread_weight(down_w, home, column, columns)
    cot_own = send(cot, swap_rule)
    cot_full = gather4(cot_own)

    resid_full = full.astype(F32)
    hat1, rstd1 = norm_parts(resid_full)
    normed1 = (hat1 * norm1_gain + norm1_shift).astype(BF)
    q = (mm(normed1, w_qkv[0]) + b_q).astype(BF)
    k = mm(normed1, w_qkv[1]).astype(BF)
    v = (mm(normed1, w_qkv[2]) + b_v).astype(BF)
    attended, lse = attn_fwd(meta, start, q, k, v, shard)

    mid = own.astype(F32) + scatter4(mm(attended, w_out)) + out_bias
    hat2, rstd2 = norm_parts(mid)
    normed2 = gather4((hat2 * norm2_gain + norm2_shift).astype(BF))
    inner = mm(normed2, w_up) + b_up
    c0 = math.sqrt(2.0 / math.pi)
    tanh = jnp.tanh(c0 * (inner + 0.044715 * inner * inner * inner))
    active = (0.5 * inner * (1.0 + tanh)).astype(BF)
    slope = 0.5 * (1.0 + tanh) + 0.5 * inner * (1.0 - tanh * tanh) * c0 * (
        1.0 + 3 * 0.044715 * inner * inner
    )
    grad_inner = (mm_nt(cot_full, w_down) * slope).astype(BF)
    grad_normed2 = scatter4(mm_nt(grad_inner, w_up))
    grad_out = cot_own.astype(F32)
    grad_mid = grad_out + norm_back(grad_normed2, hat2, rstd2, norm2_gain)
    gm_full = gather4(grad_mid.astype(BF))

    output = mid + scatter4(mm(active, w_down)) + down_bias
    output = send(output.astype(BF), swap_rule)
    up_grad = mm_tn(normed2, grad_inner).astype(BF)
    down_grad = mm_tn(active, cot_full).astype(BF)
    mlp_grad = reduce_grad(jnp.concatenate([up_grad, down_grad], axis=0), home, column, columns)

    grad_attended = mm_nt(gm_full, w_out).astype(BF)
    out_grad = reduce_grad(mm_tn(attended, gm_full).astype(BF), home, column, columns)
    dq, dk, dv = attn_bwd(meta, start, q, k, v, attended, grad_attended, lse, shard)
    part1 = mm_nt(dq, w_qkv[0]) + mm_nt(dk, w_qkv[1]) + mm_nt(dv, w_qkv[2])
    grad_normed1 = scatter4(part1)
    hat1_own, rstd1_own = norm_parts(own.astype(F32))
    input_grad = grad_mid + norm_back(grad_normed1, hat1_own, rstd1_own, norm1_gain)
    input_grad = send(input_grad.astype(BF), swap_rule)
    qkv_grad = jnp.concatenate(
        [mm_tn(normed1, dq), mm_tn(normed1, dk), mm_tn(normed1, dv)], axis=0
    ).astype(BF)
    qkv_grad = reduce_grad(qkv_grad, home, column, columns).reshape(3, model, width)

    quarter_bias = jnp.concatenate(
        [
            jnp.sum(dq, axis=0, dtype=F32),
            jnp.sum(dv, axis=0, dtype=F32),
            jnp.sum(grad_inner, axis=0, dtype=F32),
        ]
    )
    slots = lax.broadcasted_iota(jnp.int32, (4, 1), 0) == rank
    small = jnp.concatenate(
        [
            jnp.sum(part1 * hat1, axis=0),
            jnp.sum(part1, axis=0),
            jnp.sum(grad_mid, axis=0),
            jnp.sum(grad_normed2 * hat2, axis=0),
            jnp.sum(grad_normed2, axis=0),
            jnp.sum(grad_out, axis=0),
            jnp.where(slots, quarter_bias[None], 0.0).reshape(-1),
        ]
    )
    small = sum_all(small)
    gain1, shift1, out_b, gain2, shift2, down_b = [
        small[i * model : (i + 1) * model] for i in range(6)
    ]
    split = 2 * width + hidden_units
    quarter = lax.dynamic_slice_in_dim(small, 6 * model + t * split, split, 0)
    return (
        output[None],
        input_grad[None],
        gain1,
        shift1,
        qkv_grad,
        quarter[: 2 * width].reshape(2, width),
        out_grad,
        out_b,
        gain2,
        shift2,
        mlp_grad[:model],
        quarter[2 * width :],
        mlp_grad[model:],
        down_b,
    )


def solution(mesh):
    in_specs = (
        P("dp", "tensor", None),
        P("dp", None),
        P("dp"),
        P(),
        P(),
        P(None, None, "tensor"),
        P(None, "tensor"),
        P("tensor", None),
        P(),
        P(),
        P(),
        P(None, "tensor"),
        P("tensor"),
        P("tensor", None),
        P(),
        P("dp", "tensor", None),
    )
    out_specs = (
        P("dp", "tensor", None),
        P("dp", "tensor", None),
        P(),
        P(),
        P(None, None, "tensor"),
        P(None, "tensor"),
        P("tensor", None),
        P(),
        P(),
        P(),
        P(None, "tensor"),
        P("tensor"),
        P("tensor", None),
        P(),
    )
    return jax.shard_map(body, mesh=mesh, in_specs=in_specs, out_specs=out_specs, check_vma=False)
```

time: 1790 us -> 725 us (0.41)
  waiting for transfers between devices: 897 us -> 137 us
  blocking collectives: 336 us -> 0 us
  starting transfers between devices: 1.26 us -> 161 us
  local copies, waits for them, and re-layouts: 287 us -> 172 us
  matrix products: 170 us -> 81.7 us
  other arithmetic: 65.4 us -> 119 us
  Pallas kernels: 0 us -> 37.6 us
    unnamed x14 -> x0, waiting for transfers between devices: 706 us -> none
    unnamed x1 -> x0, blocking collectives: 297 us -> none
    all_gather x4 -> x0, waiting for transfers between devices: 191 us -> none  [the longest x1 58.4 us: body(): lax.all_gather(normed2.astype(jnp.bfloat16), 'tensor', axis=1, tiled=True)]
    ppermute x0 -> x80, starting transfers between devices: none -> 161 us  [send(): return lax.ppermute(x, AXES, pairs)]
    ppermute x0 -> x80, waiting for transfers between devices: none -> 137 us  [send(): return lax.ppermute(x, AXES, pairs)]
    concatenate x1 -> x9, local copies, waits for them, and re-layouts: 123 us -> 31.2 us  [the longest x4 18.9 us: gather4(): return jnp.concatenate([x, xz, xc, xzc], axis=0)]
    dot_general x18, matrix products: 170 us -> 81.7 us  [the longest x6 37.3 us: mm_nt(): lax.dot_general(a, b, (((1,), (1,)), ((), ())), preferred_element_type=F32)]
    psum x1 -> x0, blocking collectives: 39.7 us -> none  [body(): lax.psum((norm1_gain_grad, norm1_shift_grad, out_bias_grad, norm2_gain_gr...]
  transfers between devices with their start and end apart: 9 -> 80, of which waited for: 9 -> 20; matrix products, arithmetic and copies ran while one was open for 8% -> 44% of each run, Pallas kernels for 0% -> 5%
where the time goes in v1:
time: 725 us; the launch traced here: 712 us
  local copies, waits for them, and re-layouts  172 us (24%)
  starting transfers between devices  161 us (22%)
  waiting for transfers between devices  137 us (19%)
  other arithmetic  119 us (16%)
  matrix products  81.7 us (11%)
  Pallas kernels  37.6 us (5%)
    ppermute x80, starting transfers between devices, send(): return lax.ppermute(x, AXES, pairs)  161 us
    ppermute x80, waiting for transfers between devices, send(): return lax.ppermute(x, AXES, pairs)  137 us
    dot_general x6, matrix products, mm_nt(): lax.dot_general(a, b, (((1,), (1,)), ((), ())), preferred_element_type=F32)  37.3 us
    ppermute x15, local copies, waits for them, and re-layouts, send(): return lax.ppermute(x, AXES, pairs)  31.3 us
    dynamic_update_slice x4, local copies, waits for them, and re-layouts, spread_weight(): lax.dynamic_update_slice_in_dim(whole, jnp.where(home, piece(index), got)...  24.7 us
    dot_general x6, matrix products, mm(): return jnp.dot(a, b, preferred_element_type=F32)  23.2 us
    unnamed x146, local copies, waits for them, and re-layouts  22.9 us
    pallas_call x1, Pallas kernels, attn_bwd(): pl.pallas_call(functools.partial(attn_bwd_kernel, heads, shard), out_shap...  22.1 us
  transfers between devices with their start and end apart: 80, of which 20 were waited for; matrix products, arithmetic and copies ran while one was open for 44% of the time, Pallas kernels for 5%

profile of v1, /device:TPU:1, one launch (start us, length us, event | category | flops | bytes accessed | tf_op | source)
XLA Modules:
  0.0 711.7 jit_solution(6870347029711892870)
XLA Ops:
  2.0 5.6 collective-permute-start.1
  15.1 3.2 concatenate.67
  25.3 16.4 %collective-permute-done.5 = bf16[840,280]{0,1:T(8,128)(2,1)} collective-permute-done((bf16[840,280]{0,1:T(8,128)(2,1)}, bf16[840,280]{0,1:T(8,128)(2,1)}, u32[]{:S(2)}, u32[]{:S(2)}) %collective-permute-start.5) | collective-permute-done | bytes 470432 | tf_op jit(solution)/shard_map/ppermute | solution.py:273
  45.2 5.8 dynamic_update_slice.48
  51.0 4.4 collective-permute-start.8
  71.9 5.3 collective-permute-done.10
  83.0 5.8 collective-permute-start.2
  88.8 3.5 collective-permute-start.11
  92.3 3.5 dynamic-slice_select_fusion
  95.8 6.4 dynamic_update_slice.49
  102.2 6.4 dynamic_update_slice.50
  108.6 6.1 dynamic_update_slice.51
  124.6 3.7 collective-permute-done.13
  140.4 3.8 collective-permute-start.20
  146.8 5.1 concatenate.66
  154.8 3.0 convolution_convert_fusion.5.k
  157.8 3.0 fusion.16.v
  163.7 15.5 %attn_fwd.1 = (bf16[1280,280]{1,0:T(8,128)(2,1)}, f32[8,1280]{1,0:T(8,128)}) custom-call(s32[6]{0:T(128)} %pad_add_fusion.1.meta, s32[1,1280]{1,0:T(1,128)} %broadcast_in_dim.26.start, bf16[1280,280]{1,0:T(8,128)(2,1)} %fusion.15.q, bf16[1280,280]{1,0:T(8,128)(2,1)} %convolution_convert_fusion.5.k, bf16[1280,280]{1,0:T(8,128)(2,1)} %fusion.16.v), custom_call_target="tpu_custom_call" | custom-call | flops 1376256000 | bytes 5734400 | tf_op jit(solution)/shard_map/attn_fwd/pallas_call | solution.py:209
  179.2 3.1 convolution_convert_fusion.2
  187.3 4.3 collective-permute-start.24
  205.4 3.2 add_convert_fusion.7
  210.9 4.5 collective-permute-done.21
  221.4 12.8 %collective-permute-done.15 = bf16[320,1120]{1,0:T(8,128)(2,1)} collective-permute-done((bf16[320,1120]{1,0:T(8,128)(2,1)}, bf16[320,1120]{1,0:T(8,128)(2,1)}, u32[]{:S(2)}, u32[]{:S(2)}) %collective-permute-start.15) | collective-permute-done | bytes 716832 | tf_op jit(solution)/shard_map/ppermute | solution.py:273
  245.9 4.1 collective-permute-done.31
  252.6 9.4 %collective-permute-done.16 = bf16[320,1120]{1,0:T(8,128)(2,1)} collective-permute-done((bf16[320,1120]{1,0:T(8,128)(2,1)}, bf16[320,1120]{1,0:T(8,128)(2,1)}, u32[]{:S(2)}, u32[]{:S(2)}) %collective-permute-start.16) | collective-permute-done | bytes 716832 | tf_op jit(solution)/shard_map/ppermute | solution.py:273
  273.6 6.5 concatenate.69
  280.0 6.9 convolution_add_fusion.1
  287.0 7.1 convolution_convert_fusion
  294.1 8.9 %convert_reduce_fusion.2 = (f32[1120]{0:T(1024)}, bf16[1280,1120]{0,1:T(8,128)(2,1)S(1)}) fusion(f32[1280,1120]{0,1:T(8,128)S(1)} %convolution_add_fusion.1, bf16[1280,1120]{1,0:T(8,128)(2,1)} %constant_dynamic-update-slice_fusion, bf16[1120,1120]{1,0:T(8,128)(2,1)S(1)} %copy-done.43), kind=kOutput, calls=%fused_computation.28 | convolution fusion | flops 3241368576 | bytes 13982080 | tf_op jit(solution)/shard_map/dot_general | solution.py:386
  303.0 4.4 convolution_convert_fusion.4
  308.7 4.3 convolution_convert_fusion.1
  314.7 5.6 convolution_convert_fusion.3
  323.4 13.5 %collective-permute-done.74 = bf16[560,1120]{1,0:T(8,128)(2,1)S(1)} collective-permute-done((bf16[560,1120]{1,0:T(8,128)(2,1)S(1)}, bf16[560,1120]{1,0:T(8,128)(2,1)S(1)}, u32[]{:S(2)}, u32[]{:S(2)}) %collective-permute-start.74) | collective-permute-done | bytes 1254432 | tf_op jit(solution)/shard_map/ppermute | solution.py:273
  349.3 3.2 add_convert_fusion.3
  358.3 7.3 %collective-permute-start.76 = (bf16[280,1120]{1,0:T(8,128)(2,1)}, bf16[280,1120]{1,0:T(8,128)(2,1)}, u32[]{:S(2)}, u32[]{:S(2)}) collective-permute-start(bf16[280,1120]{1,0:T(8,128)(2,1)} %add_convert_fusion.9), channel_id=1, source_target_pairs={{2,0},{3,1},{4,6},{5,7},{10,8},{11,9},{12,14},{13,15},{18,16},{19,... | collective-permute-start | bytes 1881608 | tf_op jit(solution)/shard_map/ppermute | solution.py:273
  369.2 24.9 %collective-permute-done.35 = bf16[320,1120]{1,0:T(8,128)(2,1)} collective-permute-done((bf16[320,1120]{1,0:T(8,128)(2,1)}, bf16[320,1120]{1,0:T(8,128)(2,1)}, u32[]{:S(2)}, u32[]{:S(2)}) %collective-permute-start.35) | collective-permute-done | bytes 716832 | tf_op jit(solution)/shard_map/ppermute | solution.py:273
  396.3 3.9 multiply_reduce_fusion
  402.4 6.2 fusion.49
  412.9 4.0 collective-permute-start.37
  419.1 6.7 collective-permute-start.29
  433.1 8.3 %collective-permute-done.29 = bf16[320,1120]{1,0:T(8,128)(2,1)} collective-permute-done((bf16[320,1120]{1,0:T(8,128)(2,1)}, bf16[320,1120]{1,0:T(8,128)(2,1)}, u32[]{:S(2)}, u32[]{:S(2)}) %collective-permute-start.29) | collective-permute-done | bytes 716832 | tf_op jit(solution)/shard_map/ppermute | solution.py:273
  459.9 6.4 concatenate.71
  466.3 4.1 convolution_convert_fusion.6
  474.9 22.1 %attn_bwd.1 = (bf16[1280,280]{1,0:T(8,128)(2,1)}, bf16[1280,280]{1,0:T(8,128)(2,1)}, bf16[1280,280]{1,0:T(8,128)(2,1)}) custom-call(s32[6]{0:T(128)} %pad_add_fusion.1.meta, s32[1,1280]{1,0:T(1,128)} %broadcast_in_dim.26.start, bf16[1280,280]{1,0:T(8,128)(2,1)} %fusion.15.q, bf16[1280,280]{1,0:T(8,128)(2,1)} %convolution_convert_fusion.5.k, ...), custom_call_target="tpu_custom_call" | custom-call | flops 3670016000 | bytes 5734400 | tf_op jit(solution)/shard_map/attn_bwd/pallas_call | solution.py:238
  498.4 3.4 convolution_convert_fusion.10
  504.1 4.5 fusion.30
  510.6 4.5 fusion.33
  517.8 4.4 collective-permute-start.58
  523.9 9.7 %fusion.48 = (f32[1120]{0:T(1024)}, f32[1120]{0:T(1024)}, bf16[1280,1120]{0,1:T(8,128)(2,1)}) fusion(f32[1280]{0:T(1024)} %copy-done.59, f32[1280]{0:T(1024)S(1)} %broadcast_multiply_fusion, bf16[1280,1120]{0,1:T(8,128)(2,1)S(1)} %concatenate.66, f32[1280,1120]{0,1:T(8,128)} %fusion.30, f32[1280,1120]{0,1:T(8,128)} %fusion.33, ...), kind=kOutput, calls=%fused_computation.212 | convolution fusion | flops 815716096 | bytes 18853632 | tf_op jit(solution)/shard_map/dot_general | solution.py:386
  536.9 4.4 concatenate.76
  558.3 6.3 collective-permute-done.64
  565.3 4.9 collective-permute-start.65
  572.7 3.4 collective-permute-start.60
  580.2 16.0 %collective-permute-start.39 = (bf16[640,1120]{0,1:T(8,128)(2,1)}, bf16[640,1120]{0,1:T(8,128)(2,1)S(1)}, u32[]{:S(2)}, u32[]{:S(2)}) collective-permute-start(bf16[640,1120]{0,1:T(8,128)(2,1)} %slice.238), channel_id=1, source_target_pairs={{0,4},{1,5},{2,6},{3,7},{4,0},{5,1},{6,2},{7,3},{8,12},{9,13},{10,... | collective-permute-start | bytes 4300808 | tf_op jit(solution)/shard_map/ppermute | solution.py:273
  616.8 3.4 pad_maximum_fusion
  641.5 3.1 concatenate.78
  651.0 3.0 fusion.25
  655.7 11.9 %collective-permute-start.41 = (bf16[320,1120]{1,0:T(8,128)(2,1)S(1)}, bf16[320,1120]{1,0:T(8,128)(2,1)S(1)}, u32[]{:S(2)}, u32[]{:S(2)}) collective-permute-start(bf16[320,1120]{1,0:T(8,128)(2,1)S(1)} %copy.139), channel_id=1, source_target_pairs={{0,0},{1,1},{2,4},{3,5},{4,2},{5,3},{6,6},{7,7},{8,8},{9,9},{10,12... | collective-permute-start | bytes 2150408 | tf_op jit(solution)/shard_map/ppermute | solution.py:273
  670.5 14.1 %collective-permute-done.41 = bf16[320,1120]{1,0:T(8,128)(2,1)S(1)} collective-permute-done((bf16[320,1120]{1,0:T(8,128)(2,1)S(1)}, bf16[320,1120]{1,0:T(8,128)(2,1)S(1)}, u32[]{:S(2)}, u32[]{:S(2)}) %collective-permute-start.41) | collective-permute-done | bytes 716832 | tf_op jit(solution)/shard_map/ppermute | solution.py:273
  684.6 3.7 select_convert_fusion.1
  688.3 6.9 reshape.134
  695.2 4.8 copy.140
  700.0 3.9 select_convert_fusion
  703.9 4.7 fusion.52
  (436 shorter events, 285.6 us)
Async XLA Ops:
  2.0 19.2 %collective-permute-start.1 = (s32[1281]{0:T(1024)S(1)}, s32[1281]{0:T(1024)S(1)}, u32[]{:S(2)}, u32[]{:S(2)}) collective-permute-start(s32[1281]{0:T(1024)S(1)} %pad_add_fusion), channel_id=1, source_target_pairs={{0,0},{1,1},{2,4},{3,5},{4,2},{5,3},{6,6},{7,7},{8,8},{9,9},{10,12... | collective-permute-start | bytes 15380 | tf_op jit(solution)/shard_map/ppermute | solution.py:273
  9.2 15.3 %collective-permute-start.9 = (f32[1680]{0:T(1024)S(1)}, f32[1680]{0:T(1024)S(1)}, u32[]{:S(2)}, u32[]{:S(2)}) collective-permute-start(f32[1680]{0:T(1024)S(1)} %pad_maximum_fusion.10), channel_id=1, source_target_pairs={{0,2},{1,3},{6,4},{7,5},{8,10},{9,11},{14,12},{15,13},{16,18},{17,... | collective-permute-start | bytes 20168 | tf_op jit(solution)/shard_map/ppermute | solution.py:273
  10.4 49.3 %collective-permute-start = (bf16[320,1120]{1,0:T(8,128)(2,1)}, bf16[320,1120]{1,0:T(8,128)(2,1)S(1)}, u32[]{:S(2)}, u32[]{:S(2)}) collective-permute-start(bf16[320,1120]{1,0:T(8,128)(2,1)} %bitcast.43), channel_id=1, source_target_pairs={{0,0},{1,1},{2,4},{3,5},{4,2},{5,3},{6,6},{7,7},{8,8},{9,9},{10,12... | collective-permute-start | bytes 2150408 | tf_op jit(solution)/shard_map/ppermute | solution.py:273
  19.3 22.4 %collective-permute-start.5 = (bf16[840,280]{0,1:T(8,128)(2,1)}, bf16[840,280]{0,1:T(8,128)(2,1)}, u32[]{:S(2)}, u32[]{:S(2)}) collective-permute-start(bf16[840,280]{0,1:T(8,128)(2,1)} %constant_dynamic-slice_fusion.13), channel_id=1, source_target_pairs={{0,2},{1,3},{6,4},{7,5},{8,10},{9,11},{14,12},{15,13},{16,18},{17,... | collective-permute-start | bytes 1411208 | tf_op jit(solution)/shard_map/ppermute | solution.py:273
  51.0 30.1 %collective-permute-start.8 = (bf16[840,280]{0,1:T(8,128)(2,1)}, bf16[840,280]{0,1:T(8,128)(2,1)}, u32[]{:S(2)}, u32[]{:S(2)}) collective-permute-start(bf16[840,280]{0,1:T(8,128)(2,1)} %collective-permute-done.5), channel_id=1, source_target_pairs={{2,26},{3,27},{4,28},{5,29},{10,18},{11,19},{12,20},{13,21},{18,10... | collective-permute-start | bytes 1411208 | tf_op jit(solution)/shard_map/ppermute | solution.py:273
  55.4 27.6 %collective-permute-start.7 = (bf16[840,280]{0,1:T(8,128)(2,1)}, bf16[840,280]{0,1:T(8,128)(2,1)}, u32[]{:S(2)}, u32[]{:S(2)}) collective-permute-start(bf16[840,280]{0,1:T(8,128)(2,1)} %collective-permute-done.5), channel_id=1, source_target_pairs={{2,18},{3,19},{4,20},{5,21},{10,26},{11,27},{12,28},{13,29},{18,2}... | collective-permute-start | bytes 1411208 | tf_op jit(solution)/shard_map/ppermute | solution.py:273
  57.7 31.1 %collective-permute-start.6 = (bf16[840,280]{0,1:T(8,128)(2,1)}, bf16[840,280]{0,1:T(8,128)(2,1)}, u32[]{:S(2)}, u32[]{:S(2)}) collective-permute-start(bf16[840,280]{0,1:T(8,128)(2,1)} %collective-permute-done.5), channel_id=1, source_target_pairs={{2,10},{3,11},{4,12},{5,13},{10,2},{11,3},{12,4},{13,5},{18,26},{1... | collective-permute-start | bytes 1411208 | tf_op jit(solution)/shard_map/ppermute | solution.py:273
  60.6 16.6 %collective-permute-start.10 = (bf16[72,1120]{1,0:T(8,128)(2,1)}, bf16[72,1120]{1,0:T(8,128)(2,1)}, u32[]{:S(2)}, u32[]{:S(2)}) collective-permute-start(bf16[72,1120]{1,0:T(8,128)(2,1)} %pad_dynamic-slice_fusion.7), channel_id=1, source_target_pairs={{0,2},{1,3},{6,4},{7,5},{8,10},{9,11},{14,12},{15,13},{16,18},{17,... | collective-permute-start | bytes 483848 | tf_op jit(solution)/shard_map/ppermute | solution.py:273
  65.8 63.6 %collective-permute-start.23 = (bf16[280,1120]{1,0:T(8,128)(2,1)}, bf16[280,1120]{1,0:T(8,128)(2,1)}, u32[]{:S(2)}, u32[]{:S(2)}) collective-permute-start(bf16[280,1120]{1,0:T(8,128)(2,1)} %constant_dynamic-slice_fusion.11), channel_id=1, source_target_pairs={{0,2},{1,3},{6,4},{7,5},{8,10},{9,11},{14,12},{15,13},{16,18},{17,... | collective-permute-start | bytes 1881608 | tf_op jit(solution)/shard_map/ppermute | solution.py:273
  77.2 55.1 %collective-permute-start.19 = (bf16[280,1120]{1,0:T(8,128)(2,1)}, bf16[280,1120]{1,0:T(8,128)(2,1)}, u32[]{:S(2)}, u32[]{:S(2)}) collective-permute-start(bf16[280,1120]{1,0:T(8,128)(2,1)} %constant_dynamic-slice_fusion.12), channel_id=1, source_target_pairs={{0,2},{1,3},{6,4},{7,5},{8,10},{9,11},{14,12},{15,13},{16,18},{17,... | collective-permute-start | bytes 1881608 | tf_op jit(solution)/shard_map/ppermute | solution.py:273
  81.0 106.2 %collective-permute-start.30 = (bf16[320,1120]{1,0:T(8,128)(2,1)}, bf16[320,1120]{1,0:T(8,128)(2,1)}, u32[]{:S(2)}, u32[]{:S(2)}) collective-permute-start(bf16[320,1120]{1,0:T(8,128)(2,1)} %bitcast.44), channel_id=1, source_target_pairs={{0,0},{1,1},{2,4},{3,5},{4,2},{5,3},{6,6},{7,7},{8,8},{9,9},{10,12... | collective-permute-start | bytes 2150408 | tf_op jit(solution)/shard_map/ppermute | solution.py:273
  83.0 45.3 %collective-permute-start.2 = (bf16[320,1120]{1,0:T(8,128)(2,1)}, bf16[320,1120]{1,0:T(8,128)(2,1)}, u32[]{:S(2)}, u32[]{:S(2)}) collective-permute-start(bf16[320,1120]{1,0:T(8,128)(2,1)} %copy-done.36), channel_id=1, source_target_pairs={{0,1},{1,0},{2,3},{3,2},{4,5},{5,4},{6,7},{7,6},{8,9},{9,8},{10,11... | collective-permute-start | bytes 2150408 | tf_op jit(solution)/shard_map/ppermute | solution.py:273
  88.8 26.0 %collective-permute-start.11 = (bf16[72,1120]{1,0:T(8,128)(2,1)}, bf16[72,1120]{1,0:T(8,128)(2,1)}, u32[]{:S(2)}, u32[]{:S(2)}) collective-permute-start(bf16[72,1120]{1,0:T(8,128)(2,1)} %collective-permute-done.10), channel_id=1, source_target_pairs={{2,10},{3,11},{4,12},{5,13},{10,2},{11,3},{12,4},{13,5},{18,26},{1... | collective-permute-start | bytes 483848 | tf_op jit(solution)/shard_map/ppermute | solution.py:273
  128.2 12.1 %collective-permute-start.3 = (bf16[320,1120]{1,0:T(8,128)(2,1)S(1)}, bf16[320,1120]{1,0:T(8,128)(2,1)S(1)}, u32[]{:S(2)}, u32[]{:S(2)}) collective-permute-start(bf16[320,1120]{1,0:T(8,128)(2,1)S(1)} %copy-done.37), channel_id=1, source_target_pairs={{0,4},{1,5},{2,6},{3,7},{4,0},{5,1},{6,2},{7,3},{8,12},{9,13},{10,... | collective-permute-start | bytes 2150408 | tf_op jit(solution)/shard_map/ppermute | solution.py:273
  128.2 17.3 %collective-permute-start.4 = (bf16[320,1120]{1,0:T(8,128)(2,1)}, bf16[320,1120]{1,0:T(8,128)(2,1)S(1)}, u32[]{:S(2)}, u32[]{:S(2)}) collective-permute-start(bf16[320,1120]{1,0:T(8,128)(2,1)} %collective-permute-done.2), channel_id=1, source_target_pairs={{0,4},{1,5},{2,6},{3,7},{4,0},{5,1},{6,2},{7,3},{8,12},{9,13},{10,... | collective-permute-start | bytes 2150408 | tf_op jit(solution)/shard_map/ppermute | solution.py:273
  129.5 120.6 %collective-permute-start.26 = (bf16[280,1120]{1,0:T(8,128)(2,1)}, bf16[280,1120]{1,0:T(8,128)(2,1)}, u32[]{:S(2)}, u32[]{:S(2)}) collective-permute-start(bf16[280,1120]{1,0:T(8,128)(2,1)} %collective-permute-done.23), channel_id=1, source_target_pairs={{2,26},{3,27},{4,28},{5,29},{10,18},{11,19},{12,20},{13,21},{18,10... | collective-permute-start | bytes 1881608 | tf_op jit(solution)/shard_map/ppermute | solution.py:273
  132.3 85.4 %collective-permute-start.25 = (bf16[280,1120]{1,0:T(8,128)(2,1)}, bf16[280,1120]{1,0:T(8,128)(2,1)}, u32[]{:S(2)}, u32[]{:S(2)}) collective-permute-start(bf16[280,1120]{1,0:T(8,128)(2,1)} %collective-permute-done.23), channel_id=1, source_target_pairs={{2,18},{3,19},{4,20},{5,21},{10,26},{11,27},{12,28},{13,29},{18,2}... | collective-permute-start | bytes 1881608 | tf_op jit(solution)/shard_map/ppermute | solution.py:273
  140.4 55.4 %collective-permute-start.20 = (bf16[280,1120]{1,0:T(8,128)(2,1)}, bf16[280,1120]{1,0:T(8,128)(2,1)}, u32[]{:S(2)}, u32[]{:S(2)}) collective-permute-start(bf16[280,1120]{1,0:T(8,128)(2,1)} %collective-permute-done.19), channel_id=1, source_target_pairs={{2,10},{3,11},{4,12},{5,13},{10,2},{11,3},{12,4},{13,5},{18,26},{1... | collective-permute-start | bytes 1881608 | tf_op jit(solution)/shard_map/ppermute | solution.py:273
  183.7 21.7 %collective-permute-start.14 = (bf16[640,1120]{0,1:T(8,128)(2,1)}, bf16[640,1120]{0,1:T(8,128)(2,1)}, u32[]{:S(2)}, u32[]{:S(2)}) collective-permute-start(bf16[640,1120]{0,1:T(8,128)(2,1)} %slice.222), channel_id=1, source_target_pairs={{0,4},{1,5},{2,6},{3,7},{4,0},{5,1},{6,2},{7,3},{8,12},{9,13},{10,... | collective-permute-start | bytes 4300808 | tf_op jit(solution)/shard_map/ppermute | solution.py:273
  187.3 13.6 %collective-permute-start.24 = (bf16[280,1120]{1,0:T(8,128)(2,1)}, bf16[280,1120]{1,0:T(8,128)(2,1)}, u32[]{:S(2)}, u32[]{:S(2)}) collective-permute-start(bf16[280,1120]{1,0:T(8,128)(2,1)} %collective-permute-done.23), channel_id=1, source_target_pairs={{2,10},{3,11},{4,12},{5,13},{10,2},{11,3},{12,4},{13,5},{18,26},{1... | collective-permute-start | bytes 1881608 | tf_op jit(solution)/shard_map/ppermute | solution.py:273
  195.8 48.1 %collective-permute-start.22 = (bf16[280,1120]{1,0:T(8,128)(2,1)}, bf16[280,1120]{1,0:T(8,128)(2,1)S(1)}, u32[]{:S(2)}, u32[]{:S(2)}) collective-permute-start(bf16[280,1120]{1,0:T(8,128)(2,1)} %collective-permute-done.19), channel_id=1, source_target_pairs={{2,26},{3,27},{4,28},{5,29},{10,18},{11,19},{12,20},{13,21},{18,10... | collective-permute-start | bytes 1881608 | tf_op jit(solution)/shard_map/ppermute | solution.py:273
  200.9 14.5 %collective-permute-start.21 = (bf16[280,1120]{1,0:T(8,128)(2,1)}, bf16[280,1120]{1,0:T(8,128)(2,1)}, u32[]{:S(2)}, u32[]{:S(2)}) collective-permute-start(bf16[280,1120]{1,0:T(8,128)(2,1)} %collective-permute-done.19), channel_id=1, source_target_pairs={{2,18},{3,19},{4,20},{5,21},{10,26},{11,27},{12,28},{13,29},{18,2}... | collective-permute-start | bytes 1881608 | tf_op jit(solution)/shard_map/ppermute | solution.py:273
  205.4 58.7 %collective-permute-start.32 = (bf16[320,1120]{1,0:T(8,128)(2,1)}, bf16[320,1120]{1,0:T(8,128)(2,1)}, u32[]{:S(2)}, u32[]{:S(2)}) collective-permute-start(bf16[320,1120]{1,0:T(8,128)(2,1)} %collective-permute-done.30), channel_id=1, source_target_pairs={{0,4},{1,5},{2,6},{3,7},{4,0},{5,1},{6,2},{7,3},{8,12},{9,13},{10,... | collective-permute-start | bytes 2150408 | tf_op jit(solution)/shard_map/ppermute | solution.py:273
  215.4 18.8 %collective-permute-start.15 = (bf16[320,1120]{1,0:T(8,128)(2,1)}, bf16[320,1120]{1,0:T(8,128)(2,1)}, u32[]{:S(2)}, u32[]{:S(2)}) collective-permute-start(bf16[320,1120]{1,0:T(8,128)(2,1)} %copy.118), channel_id=1, source_target_pairs={{0,1},{1,0},{2,3},{3,2},{4,5},{5,4},{6,7},{7,6},{8,9},{9,8},{10,11... | collective-permute-start | bytes 2150408 | tf_op jit(solution)/shard_map/ppermute | solution.py:273
  217.7 32.3 %collective-permute-start.31 = (bf16[320,1120]{1,0:T(8,128)(2,1)}, bf16[320,1120]{1,0:T(8,128)(2,1)}, u32[]{:S(2)}, u32[]{:S(2)}) collective-permute-start(bf16[320,1120]{1,0:T(8,128)(2,1)} %collective-permute-done.30), channel_id=1, source_target_pairs={{0,1},{1,0},{2,3},{3,2},{4,5},{5,4},{6,7},{7,6},{8,9},{9,8},{10,11... | collective-permute-start | bytes 2150408 | tf_op jit(solution)/shard_map/ppermute | solution.py:273
  243.8 18.2 %collective-permute-start.16 = (bf16[320,1120]{1,0:T(8,128)(2,1)}, bf16[320,1120]{1,0:T(8,128)(2,1)}, u32[]{:S(2)}, u32[]{:S(2)}) collective-permute-start(bf16[320,1120]{1,0:T(8,128)(2,1)} %copy.120), channel_id=1, source_target_pairs={{0,1},{1,0},{2,3},{3,2},{4,5},{5,4},{6,7},{7,6},{8,9},{9,8},{10,11... | collective-permute-start | bytes 2150408 | tf_op jit(solution)/shard_map/ppermute | solution.py:273
  250.0 16.1 %collective-permute-start.33 = (bf16[320,1120]{1,0:T(8,128)(2,1)}, bf16[320,1120]{1,0:T(8,128)(2,1)S(1)}, u32[]{:S(2)}, u32[]{:S(2)}) collective-permute-start(bf16[320,1120]{1,0:T(8,128)(2,1)} %collective-permute-done.31), channel_id=1, source_target_pairs={{0,4},{1,5},{2,6},{3,7},{4,0},{5,1},{6,2},{7,3},{8,12},{9,13},{10,... | collective-permute-start | bytes 2150408 | tf_op jit(solution)/shard_map/ppermute | solution.py:273
  252.3 16.9 %collective-permute-start.17 = (bf16[320,1120]{1,0:T(8,128)(2,1)}, bf16[320,1120]{1,0:T(8,128)(2,1)}, u32[]{:S(2)}, u32[]{:S(2)}) collective-permute-start(bf16[320,1120]{1,0:T(8,128)(2,1)} %copy.120), channel_id=1, source_target_pairs={{0,4},{1,5},{2,6},{3,7},{4,0},{5,1},{6,2},{7,3},{8,12},{9,13},{10,... | collective-permute-start | bytes 2150408 | tf_op jit(solution)/shard_map/ppermute | solution.py:273
  262.0 9.4 %collective-permute-start.18 = (bf16[320,1120]{1,0:T(8,128)(2,1)}, bf16[320,1120]{1,0:T(8,128)(2,1)}, u32[]{:S(2)}, u32[]{:S(2)}) collective-permute-start(bf16[320,1120]{1,0:T(8,128)(2,1)} %collective-permute-done.16), channel_id=1, source_target_pairs={{0,4},{1,5},{2,6},{3,7},{4,0},{5,1},{6,2},{7,3},{8,12},{9,13},{10,... | collective-permute-start | bytes 2150408 | tf_op jit(solution)/shard_map/ppermute | solution.py:273
  307.5 29.4 %collective-permute-start.74 = (bf16[560,1120]{1,0:T(8,128)(2,1)S(1)}, bf16[560,1120]{1,0:T(8,128)(2,1)S(1)}, u32[]{:S(2)}, u32[]{:S(2)}) collective-permute-start(bf16[560,1120]{1,0:T(8,128)(2,1)S(1)} %constant_dynamic-slice_fusion), channel_id=1, source_target_pairs={{0,16},{1,17},{2,18},{3,19},{4,20},{5,21},{6,22},{7,23},{8,24},{9,... | collective-permute-start | bytes 3763208 | tf_op jit(solution)/shard_map/ppermute | solution.py:273
  313.1 29.2 %collective-permute-start.69 = (bf16[560,1120]{1,0:T(8,128)(2,1)S(1)}, bf16[560,1120]{1,0:T(8,128)(2,1)S(1)}, u32[]{:S(2)}, u32[]{:S(2)}) collective-permute-start(bf16[560,1120]{1,0:T(8,128)(2,1)S(1)} %constant_dynamic-slice_fusion.2), channel_id=1, source_target_pairs={{0,8},{1,9},{2,10},{3,11},{4,12},{5,13},{6,14},{7,15},{8,0},{9,1},... | collective-permute-start | bytes 3763208 | tf_op jit(solution)/shard_map/ppermute | solution.py:273
  322.4 21.9 %collective-permute-start.27 = (bf16[640,1120]{0,1:T(8,128)(2,1)S(1)}, bf16[640,1120]{0,1:T(8,128)(2,1)S(1)}, u32[]{:S(2)}, u32[]{:S(2)}) collective-permute-start(bf16[640,1120]{0,1:T(8,128)(2,1)S(1)} %slice.228), channel_id=1, source_target_pairs={{0,4},{1,5},{2,6},{3,7},{4,0},{5,1},{6,2},{7,3},{8,12},{9,13},{10,... | collective-permute-start | bytes 4300808 | tf_op jit(solution)/shard_map/ppermute | solution.py:273
  323.4 25.9 %collective-permute-start.34 = (bf16[640,1120]{0,1:T(8,128)(2,1)}, bf16[640,1120]{0,1:T(8,128)(2,1)}, u32[]{:S(2)}, u32[]{:S(2)}) collective-permute-start(bf16[640,1120]{0,1:T(8,128)(2,1)} %slice.233), channel_id=1, source_target_pairs={{0,4},{1,5},{2,6},{3,7},{4,0},{5,1},{6,2},{7,3},{8,12},{9,13},{10,... | collective-permute-start | bytes 4300808 | tf_op jit(solution)/shard_map/ppermute | solution.py:273
  338.3 18.0 %collective-permute-start.75 = (bf16[280,1120]{1,0:T(8,128)(2,1)}, bf16[280,1120]{1,0:T(8,128)(2,1)S(1)}, u32[]{:S(2)}, u32[]{:S(2)}) collective-permute-start(bf16[280,1120]{1,0:T(8,128)(2,1)} %constant_dynamic-slice_fusion.10), channel_id=1, source_target_pairs={{0,8},{1,9},{2,10},{3,11},{4,12},{5,13},{6,14},{7,15},{8,0},{9,1},... | collective-permute-start | bytes 1881608 | tf_op jit(solution)/shard_map/ppermute | solution.py:273
  343.9 21.7 %collective-permute-start.70 = (bf16[280,1120]{1,0:T(8,128)(2,1)}, bf16[280,1120]{1,0:T(8,128)(2,1)}, u32[]{:S(2)}, u32[]{:S(2)}) collective-permute-start(bf16[280,1120]{1,0:T(8,128)(2,1)} %constant_dynamic-slice_fusion.1), channel_id=1, source_target_pairs={{0,16},{1,17},{2,18},{3,19},{4,20},{5,21},{6,22},{7,23},{8,24},{9,... | collective-permute-start | bytes 1881608 | tf_op jit(solution)/shard_map/ppermute | solution.py:273
  349.3 50.9 %collective-permute-start.28 = (bf16[320,1120]{1,0:T(8,128)(2,1)}, bf16[320,1120]{1,0:T(8,128)(2,1)}, u32[]{:S(2)}, u32[]{:S(2)}) collective-permute-start(bf16[320,1120]{1,0:T(8,128)(2,1)} %copy.125), channel_id=1, source_target_pairs={{0,1},{1,0},{2,3},{3,2},{4,5},{5,4},{6,7},{7,6},{8,9},{9,8},{10,11... | collective-permute-start | bytes 2150408 | tf_op jit(solution)/shard_map/ppermute | solution.py:273
  354.7 39.4 %collective-permute-start.35 = (bf16[320,1120]{1,0:T(8,128)(2,1)}, bf16[320,1120]{1,0:T(8,128)(2,1)}, u32[]{:S(2)}, u32[]{:S(2)}) collective-permute-start(bf16[320,1120]{1,0:T(8,128)(2,1)} %copy.129), channel_id=1, source_target_pairs={{0,1},{1,0},{2,3},{3,2},{4,5},{5,4},{6,7},{7,6},{8,9},{9,8},{10,11... | collective-permute-start | bytes 2150408 | tf_op jit(solution)/shard_map/ppermute | solution.py:273
  358.3 67.5 %collective-permute-start.76 = (bf16[280,1120]{1,0:T(8,128)(2,1)}, bf16[280,1120]{1,0:T(8,128)(2,1)}, u32[]{:S(2)}, u32[]{:S(2)}) collective-permute-start(bf16[280,1120]{1,0:T(8,128)(2,1)} %add_convert_fusion.9), channel_id=1, source_target_pairs={{2,0},{3,1},{4,6},{5,7},{10,8},{11,9},{12,14},{13,15},{18,16},{19,... | collective-permute-start | bytes 1881608 | tf_op jit(solution)/shard_map/ppermute | solution.py:273
  367.1 63.1 %collective-permute-start.71 = (bf16[280,1120]{1,0:T(8,128)(2,1)S(1)}, bf16[280,1120]{1,0:T(8,128)(2,1)}, u32[]{:S(2)}, u32[]{:S(2)}) collective-permute-start(bf16[280,1120]{1,0:T(8,128)(2,1)S(1)} %add_convert_fusion.11), channel_id=1, source_target_pairs={{2,0},{3,1},{4,6},{5,7},{10,8},{11,9},{12,14},{13,15},{18,16},{19,... | collective-permute-start | bytes 1881608 | tf_op jit(solution)/shard_map/ppermute | solution.py:273
  412.9 33.3 %collective-permute-start.37 = (bf16[320,1120]{1,0:T(8,128)(2,1)}, bf16[320,1120]{1,0:T(8,128)(2,1)}, u32[]{:S(2)}, u32[]{:S(2)}) collective-permute-start(bf16[320,1120]{1,0:T(8,128)(2,1)} %copy.131), channel_id=1, source_target_pairs={{0,4},{1,5},{2,6},{3,7},{4,0},{5,1},{6,2},{7,3},{8,12},{9,13},{10,... | collective-permute-start | bytes 2150408 | tf_op jit(solution)/shard_map/ppermute | solution.py:273
  416.9 26.3 %collective-permute-start.36 = (bf16[320,1120]{1,0:T(8,128)(2,1)}, bf16[320,1120]{1,0:T(8,128)(2,1)}, u32[]{:S(2)}, u32[]{:S(2)}) collective-permute-start(bf16[320,1120]{1,0:T(8,128)(2,1)} %copy.131), channel_id=1, source_target_pairs={{0,1},{1,0},{2,3},{3,2},{4,5},{5,4},{6,7},{7,6},{8,9},{9,8},{10,11... | collective-permute-start | bytes 2150408 | tf_op jit(solution)/shard_map/ppermute | solution.py:273
  419.1 22.4 %collective-permute-start.29 = (bf16[320,1120]{1,0:T(8,128)(2,1)}, bf16[320,1120]{1,0:T(8,128)(2,1)}, u32[]{:S(2)}, u32[]{:S(2)}) collective-permute-start(bf16[320,1120]{1,0:T(8,128)(2,1)} %copy.127), channel_id=1, source_target_pairs={{0,0},{1,1},{2,4},{3,5},{4,2},{5,3},{6,6},{7,7},{8,8},{9,9},{10,12... | collective-permute-start | bytes 2150408 | tf_op jit(solution)/shard_map/ppermute | solution.py:273
  428.1 20.3 %collective-permute-start.77 = (bf16[280,1120]{1,0:T(8,128)(2,1)}, bf16[280,1120]{1,0:T(8,128)(2,1)}, u32[]{:S(2)}, u32[]{:S(2)}) collective-permute-start(bf16[280,1120]{1,0:T(8,128)(2,1)} %add_convert_fusion.8), channel_id=1, source_target_pairs={{0,8},{1,9},{6,14},{7,15},{8,0},{9,1},{14,6},{15,7},{16,24},{17,25... | collective-permute-start | bytes 1881608 | tf_op jit(solution)/shard_map/ppermute | solution.py:273
  432.2 20.5 %collective-permute-start.72 = (bf16[280,1120]{1,0:T(8,128)(2,1)}, bf16[280,1120]{1,0:T(8,128)(2,1)S(1)}, u32[]{:S(2)}, u32[]{:S(2)}) collective-permute-start(bf16[280,1120]{1,0:T(8,128)(2,1)} %add_convert_fusion.10), channel_id=1, source_target_pairs={{0,16},{1,17},{6,22},{7,23},{8,24},{9,25},{14,30},{15,31},{16,0},{... | collective-permute-start | bytes 1881608 | tf_op jit(solution)/shard_map/ppermute | solution.py:273
  443.2 14.6 %collective-permute-start.38 = (bf16[320,1120]{1,0:T(8,128)(2,1)}, bf16[320,1120]{1,0:T(8,128)(2,1)}, u32[]{:S(2)}, u32[]{:S(2)}) collective-permute-start(bf16[320,1120]{1,0:T(8,128)(2,1)} %collective-permute-done.36), channel_id=1, source_target_pairs={{0,4},{1,5},{2,6},{3,7},{4,0},{5,1},{6,2},{7,3},{8,12},{9,13},{10,... | collective-permute-start | bytes 2150408 | tf_op jit(solution)/shard_map/ppermute | solution.py:273
  451.0 161.2 %collective-permute-start.78 = (bf16[560,1120]{1,0:T(8,128)(2,1)}, bf16[560,1120]{1,0:T(8,128)(2,1)}, u32[]{:S(2)}, u32[]{:S(2)}) collective-permute-start(bf16[560,1120]{1,0:T(8,128)(2,1)} %pad_maximum_fusion.2), channel_id=1, source_target_pairs={{0,16},{1,17},{6,22},{7,23},{8,24},{9,25},{14,30},{15,31},{16,0},{... | collective-permute-start | bytes 3763208 | tf_op jit(solution)/shard_map/ppermute | solution.py:273
  456.0 158.1 %collective-permute-start.73 = (bf16[560,1120]{1,0:T(8,128)(2,1)}, bf16[560,1120]{1,0:T(8,128)(2,1)}, u32[]{:S(2)}, u32[]{:S(2)}) collective-permute-start(bf16[560,1120]{1,0:T(8,128)(2,1)} %pad_maximum_fusion.1), channel_id=1, source_target_pairs={{0,8},{1,9},{6,14},{7,15},{8,0},{9,1},{14,6},{15,7},{16,24},{17,25... | collective-permute-start | bytes 3763208 | tf_op jit(solution)/shard_map/ppermute | solution.py:273
  516.0 35.3 %collective-permute-start.63 = (bf16[80,1120]{1,0:T(8,128)(2,1)}, bf16[80,1120]{1,0:T(8,128)(2,1)}, u32[]{:S(2)}, u32[]{:S(2)}) collective-permute-start(bf16[80,1120]{1,0:T(8,128)(2,1)} %constant_dynamic-slice_fusion.4), channel_id=1, source_target_pairs={{0,16},{1,17},{2,18},{3,19},{4,20},{5,21},{6,22},{7,23},{8,24},{9,... | collective-permute-start | bytes 537608 | tf_op jit(solution)/shard_map/ppermute | solution.py:273
  517.8 37.4 %collective-permute-start.58 = (bf16[80,1120]{1,0:T(8,128)(2,1)}, bf16[80,1120]{1,0:T(8,128)(2,1)}, u32[]{:S(2)}, u32[]{:S(2)}) collective-permute-start(bf16[80,1120]{1,0:T(8,128)(2,1)} %constant_dynamic-slice_fusion.6), channel_id=1, source_target_pairs={{0,8},{1,9},{2,10},{3,11},{4,12},{5,13},{6,14},{7,15},{8,0},{9,1},... | collective-permute-start | bytes 537608 | tf_op jit(solution)/shard_map/ppermute | solution.py:273
  535.0 8.0 %collective-permute-start.42 = (f32[13440]{0:T(1024)}, f32[13440]{0:T(1024)}, u32[]{:S(2)}, u32[]{:S(2)}) collective-permute-start(f32[13440]{0:T(1024)} %concatenate.73), channel_id=1, source_target_pairs={{0,4},{1,5},{2,6},{3,7},{4,0},{5,1},{6,2},{7,3},{8,12},{9,13},{10,... | collective-permute-start | bytes 161288 | tf_op jit(solution)/shard_map/ppermute | solution.py:273
  551.0 45.2 %collective-permute-start.47 = (bf16[848,280]{0,1:T(8,128)(2,1)}, bf16[848,280]{0,1:T(8,128)(2,1)}, u32[]{:S(2)}, u32[]{:S(2)}) collective-permute-start(bf16[848,280]{0,1:T(8,128)(2,1)} %fusion.38), channel_id=1, source_target_pairs={{0,8},{1,9},{2,10},{3,11},{4,12},{5,13},{6,14},{7,15},{8,0},{9,1},... | collective-permute-start | bytes 1424648 | tf_op jit(solution)/shard_map/ppermute | solution.py:273
  555.2 9.4 %collective-permute-start.64 = (bf16[40,1120]{1,0:T(8,128)(2,1)S(1)}, bf16[40,1120]{1,0:T(8,128)(2,1)S(1)}, u32[]{:S(2)}, u32[]{:S(2)}) collective-permute-start(bf16[40,1120]{1,0:T(8,128)(2,1)S(1)} %constant_dynamic-slice_fusion.3), channel_id=1, source_target_pairs={{0,8},{1,9},{2,10},{3,11},{4,12},{5,13},{6,14},{7,15},{8,0},{9,1},... | collective-permute-start | bytes 268808 | tf_op jit(solution)/shard_map/ppermute | solution.py:273
  557.5 7.8 %collective-permute-start.59 = (bf16[40,1120]{1,0:T(8,128)(2,1)S(1)}, bf16[40,1120]{1,0:T(8,128)(2,1)S(1)}, u32[]{:S(2)}, u32[]{:S(2)}) collective-permute-start(bf16[40,1120]{1,0:T(8,128)(2,1)S(1)} %constant_dynamic-slice_fusion.5), channel_id=1, source_target_pairs={{0,16},{1,17},{2,18},{3,19},{4,20},{5,21},{6,22},{7,23},{8,24},{9,... | collective-permute-start | bytes 268808 | tf_op jit(solution)/shard_map/ppermute | solution.py:273
  570.8 27.8 %collective-permute-start.52 = (bf16[848,280]{0,1:T(8,128)(2,1)}, bf16[848,280]{0,1:T(8,128)(2,1)}, u32[]{:S(2)}, u32[]{:S(2)}) collective-permute-start(bf16[848,280]{0,1:T(8,128)(2,1)} %constant_dynamic-slice_fusion.8), channel_id=1, source_target_pairs={{0,16},{1,17},{2,18},{3,19},{4,20},{5,21},{6,22},{7,23},{8,24},{9,... | collective-permute-start | bytes 1424648 | tf_op jit(solution)/shard_map/ppermute | solution.py:273
  580.2 47.8 %collective-permute-start.39 = (bf16[640,1120]{0,1:T(8,128)(2,1)}, bf16[640,1120]{0,1:T(8,128)(2,1)S(1)}, u32[]{:S(2)}, u32[]{:S(2)}) collective-permute-start(bf16[640,1120]{0,1:T(8,128)(2,1)} %slice.238), channel_id=1, source_target_pairs={{0,4},{1,5},{2,6},{3,7},{4,0},{5,1},{6,2},{7,3},{8,12},{9,13},{10,... | collective-permute-start | bytes 4300808 | tf_op jit(solution)/shard_map/ppermute | solution.py:273
  607.1 14.4 %collective-permute-start.49 = (bf16[424,280]{0,1:T(8,128)(2,1)S(1)}, bf16[424,280]{0,1:T(8,128)(2,1)S(1)}, u32[]{:S(2)}, u32[]{:S(2)}) collective-permute-start(bf16[424,280]{0,1:T(8,128)(2,1)S(1)} %add_convert_fusion.17), channel_id=1, source_target_pairs={{2,0},{3,1},{4,6},{5,7},{10,8},{11,9},{12,14},{13,15},{18,16},{19,... | collective-permute-start | bytes 712328 | tf_op jit(solution)/shard_map/ppermute | solution.py:273
  610.7 11.5 %collective-permute-start.54 = (bf16[424,280]{0,1:T(8,128)(2,1)S(1)}, bf16[424,280]{0,1:T(8,128)(2,1)S(1)}, u32[]{:S(2)}, u32[]{:S(2)}) collective-permute-start(bf16[424,280]{0,1:T(8,128)(2,1)S(1)} %add_convert_fusion.15), channel_id=1, source_target_pairs={{2,0},{3,1},{4,6},{5,7},{10,8},{11,9},{12,14},{13,15},{18,16},{19,... | collective-permute-start | bytes 712328 | tf_op jit(solution)/shard_map/ppermute | solution.py:273
  620.2 79.8 %collective-permute-start.79 = (bf16[2240,1120]{1,0:T(8,128)(2,1)}, bf16[2240,1120]{1,0:T(8,128)(2,1)}, u32[]{:S(2)}, u32[]{:S(2)}) collective-permute-start(bf16[2240,1120]{1,0:T(8,128)(2,1)} %pad_maximum_fusion), channel_id=1, source_target_pairs={{0,4},{1,5},{6,2},{7,3},{8,12},{9,13},{14,10},{15,11},{16,20},{17,... | collective-permute-start | bytes 15052808 | tf_op jit(solution)/shard_map/ppermute | solution.py:273
  624.0 14.8 %collective-permute-start.51 = (bf16[848,280]{0,1:T(8,128)(2,1)}, bf16[848,280]{0,1:T(8,128)(2,1)}, u32[]{:S(2)}, u32[]{:S(2)}) collective-permute-start(bf16[848,280]{0,1:T(8,128)(2,1)} %pad_maximum_fusion.6), channel_id=1, source_target_pairs={{0,8},{1,9},{6,14},{7,15},{8,0},{9,1},{14,6},{15,7},{16,24},{17,25... | collective-permute-start | bytes 1424648 | tf_op jit(solution)/shard_map/ppermute | solution.py:273
  626.6 13.6 %collective-permute-start.56 = (bf16[848,280]{0,1:T(8,128)(2,1)}, bf16[848,280]{0,1:T(8,128)(2,1)}, u32[]{:S(2)}, u32[]{:S(2)}) collective-permute-start(bf16[848,280]{0,1:T(8,128)(2,1)} %pad_maximum_fusion.7), channel_id=1, source_target_pairs={{0,16},{1,17},{6,22},{7,23},{8,24},{9,25},{14,30},{15,31},{16,0},{... | collective-permute-start | bytes 1424648 | tf_op jit(solution)/shard_map/ppermute | solution.py:273
  633.1 13.0 %collective-permute-start.40 = (bf16[320,1120]{1,0:T(8,128)(2,1)}, bf16[320,1120]{1,0:T(8,128)(2,1)}, u32[]{:S(2)}, u32[]{:S(2)}) collective-permute-start(bf16[320,1120]{1,0:T(8,128)(2,1)} %copy.137), channel_id=1, source_target_pairs={{0,1},{1,0},{2,3},{3,2},{4,5},{5,4},{6,7},{7,6},{8,9},{9,8},{10,11... | collective-permute-start | bytes 2150408 | tf_op jit(solution)/shard_map/ppermute | solution.py:273
  637.6 30.7 %collective-permute-start.68 = (bf16[280,1120]{1,0:T(8,128)(2,1)}, bf16[280,1120]{1,0:T(8,128)(2,1)}, u32[]{:S(2)}, u32[]{:S(2)}) collective-permute-start(bf16[280,1120]{1,0:T(8,128)(2,1)} %pad_maximum_fusion.3), channel_id=1, source_target_pairs={{0,4},{1,5},{6,2},{7,3},{8,12},{9,13},{14,10},{15,11},{16,20},{17,... | collective-permute-start | bytes 1881608 | tf_op jit(solution)/shard_map/ppermute | solution.py:273
  644.7 39.9 %collective-permute-start.57 = (bf16[3360,280]{0,1:T(8,128)(2,1)}, bf16[3360,280]{0,1:T(8,128)(2,1)}, u32[]{:S(2)}, u32[]{:S(2)}) collective-permute-start(bf16[3360,280]{0,1:T(8,128)(2,1)} %bitcast.41), channel_id=1, source_target_pairs={{0,4},{1,5},{6,2},{7,3},{8,12},{9,13},{14,10},{15,11},{16,20},{17,... | collective-permute-start | bytes 5644808 | tf_op jit(solution)/shard_map/ppermute | solution.py:273
  655.7 28.9 %collective-permute-start.41 = (bf16[320,1120]{1,0:T(8,128)(2,1)S(1)}, bf16[320,1120]{1,0:T(8,128)(2,1)S(1)}, u32[]{:S(2)}, u32[]{:S(2)}) collective-permute-start(bf16[320,1120]{1,0:T(8,128)(2,1)S(1)} %copy.139), channel_id=1, source_target_pairs={{0,0},{1,1},{2,4},{3,5},{4,2},{5,3},{6,6},{7,7},{8,8},{9,9},{10,12... | collective-permute-start | bytes 2150408 | tf_op jit(solution)/shard_map/ppermute | solution.py:273
  (86 other events, 599.9 us)

commit v2 on v1

--- a/solution.py
+++ b/solution.py
@@ -259,117 +259,407 @@
     )(meta, start, q, k, v, o, do, lse)
 
 
-AXES = ("dp", "tensor")
-
-
-def send(x, rule):
-    nd, nt = lax.axis_size("dp"), lax.axis_size("tensor")
-    pairs = []
-    for d in range(nd):
-        for t in range(nt):
-            to = rule(d, t)
-            if to is not None:
-                pairs.append((d * nt + t, to[0] * nt + to[1]))
-    return lax.ppermute(x, AXES, pairs)
-
-
-def is_home(d, t):
-    return (d & 1) == (t >> 1)
-
-
-def swap_rule(d, t):
-    return (d, t) if is_home(d, t) else (d ^ 1, t ^ 2)
-
-
-def gather4(x):
-    xz = send(x, lambda d, t: (d, t ^ 1))
-    xc = send(x, lambda d, t: (d ^ 1, t))
-    xzc = send(xz, lambda d, t: (d ^ 1, t))
-    return jnp.concatenate([x, xz, xc, xzc], axis=0)
-
-
-def scatter4(part):
-    part = part.astype(BF)
-    rows = part.shape[0] // 4
-    other = send(part[2 * rows :], lambda d, t: (d ^ 1, t))
-    far = part[rows : 2 * rows].astype(F32) + other[rows:].astype(F32)
-    far = send(far.astype(BF), lambda d, t: (d, t ^ 1))
-    return part[:rows].astype(F32) + other[:rows].astype(F32) + far.astype(F32)
-
-
-def pad_rows(x, unit):
-    extra = -x.shape[0] % unit
-    return jnp.pad(x, ((0, extra), (0, 0))) if extra else x
-
-
-def spread_weight(w, home, column, columns):
-    rows = w.shape[0]
-    w = pad_rows(w, 8 * columns)
-    unit = w.shape[0] // columns
-
-    def piece(index):
-        return lax.dynamic_slice_in_dim(w, index * unit, unit, 0)
-
-    mine = send(piece(column), lambda d, t: (d, t ^ 2) if is_home(d, t) else None)
-    whole = jnp.zeros_like(w)
-    for m in range(columns):
-        got = mine
-        if m:
-            got = send(mine, lambda d, t: None if is_home(d, t) else (d ^ (2 * m), t))
-        index = column ^ m
-        whole = lax.dynamic_update_slice_in_dim(
-            whole, jnp.where(home, piece(index), got), index * unit, 0
+MESH = pl.DeviceIdType.MESH
+CHUNKS = 2
+STEP = 32
+
+
+class Place:
+    def __init__(self, columns):
+        d, t = lax.axis_index("dp"), lax.axis_index("tensor")
+        core, low, high = lax.rem(d, 2), lax.rem(t, 2), lax.div(t, 2)
+        self.d, self.t, self.columns = d, t, columns
+        self.bits = columns.bit_length() - 1
+        self.core = (d + 1 - 2 * core, t)
+        self.near = (d, t + 1 - 2 * low)
+        self.far = (d, t + 2 - 4 * high)
+        self.swap = (d + 1 - 2 * core, t + 2 - 4 * high)
+        self.home = core == high
+        self.away = core != high
+
+    def bit(self, b):
+        return lax.rem(lax.div(self.d, 2 << b), 2)
+
+    def column(self, m):
+        d = self.d
+        for b in range(self.bits):
+            if (m >> b) & 1:
+                d = d + (2 << b) * (1 - 2 * self.bit(b))
+        return (d, self.t)
+
+
+class Link:
+    def __init__(self, send_sems, recv_sems):
+        self.send_sems, self.recv_sems = send_sems, recv_sems
+        self.count = 0
+        self.open, self.kept, self.number = [], [], {}
+
+    def make(self, src, dst, to, like=None):
+        if like is None:
+            i = self.count
+            self.count += 1
+        else:
+            i = self.number[id(like)]
+        copy = pltpu.make_async_remote_copy(
+            src_ref=src,
+            dst_ref=dst,
+            send_sem=self.send_sems.at[i],
+            recv_sem=self.recv_sems.at[i],
+            device_id=to,
+            device_id_type=MESH,
         )
-    return whole[:rows]
-
-
-def reduce_grad(g, home, column, columns):
-    rows = g.shape[0]
-    bits = columns.bit_length() - 1
-    g = pad_rows(g, 16 * columns)
-    half = g.shape[0] // 2
-    done = []
-    for side in range(2):
-        piece = g[side * half : (side + 1) * half]
-        order = [(b + side) % bits for b in range(bits)] if bits else []
-        for b in order:
-            n = piece.shape[0] // 2
-            bit = (column >> b) & 1
-            keep = lax.dynamic_slice_in_dim(piece, bit * n, n, 0)
-            away = lax.dynamic_slice_in_dim(piece, (1 - bit) * n, n, 0)
-            got = send(away, lambda d, t: (d ^ (2 << b), t))
-            piece = (keep.astype(F32) + got.astype(F32)).astype(BF)
-        got = send(piece, lambda d, t: None if is_home(d, t) else (d, t ^ 2))
-        piece = (piece.astype(F32) + got.astype(F32)).astype(BF)
-        for b in reversed(order):
-            bit = (column >> b) & 1
-            got = send(piece, lambda d, t: (d ^ (2 << b), t) if is_home(d, t) else None)
-            first = jnp.where(bit == 0, piece, got)
-            second = jnp.where(bit == 0, got, piece)
-            piece = jnp.concatenate([first, second], axis=0)
-        done.append(piece)
-    whole = jnp.concatenate(done, axis=0)[:rows]
-    other = send(whole, lambda d, t: (d ^ 1, t) if is_home(d, t) else None)
-    return jnp.where(home, whole, other).astype(F32)
-
-
-def sum_all(x):
-    for axis in range(2):
-        size = (lax.axis_size("dp"), lax.axis_size("tensor"))[axis]
-        step = 1
-        while step < size:
-            x = x + send(x, lambda d, t: (d ^ step, t) if axis == 0 else (d, t ^ step))
-            step *= 2
-    return x
-
-
-def norm_parts(values):
+        self.number[id(copy)] = i
+        self.kept.append(copy)
+        return copy
+
+    def start(self, copy, when=None):
+        if when is None:
+            copy.start()
+        else:
+            pl.when(when)(copy.start)
+        self.open.append((copy, when))
+
+    def send(self, src, dst, to, when=None):
+        copy = self.make(src, dst, to)
+        self.start(copy, when)
+        return copy
+
+    def close(self):
+        for copy, when in self.open:
+            if when is None:
+                copy.wait_send()
+            else:
+                pl.when(when)(copy.wait_send)
+
+
+def arrive(copy, when=None):
+    if when is None:
+        copy.wait_recv()
+    else:
+        pl.when(when)(copy.wait_recv)
+
+
+def meet(partners):
+    barrier = pltpu.get_barrier_semaphore()
+    for to in partners:
+        pl.semaphore_signal(barrier, inc=1, device_id=to, device_id_type=MESH)
+    pl.semaphore_wait(barrier, len(partners))
+
+
+def rows_of(ref, first, count):
+    return ref.at[pl.ds(first, count)]
+
+
+def gather_start(link, place, full, shard, i):
+    n = shard // CHUNKS
+    near = link.send(rows_of(full, i * n, n), rows_of(full, shard + i * n, n), place.near)
+    core = link.send(rows_of(full, i * n, n), rows_of(full, 2 * shard + i * n, n), place.core)
+    return near, core
+
+
+def gather_relay(link, place, full, shard, i, near):
+    n = shard // CHUNKS
+    near.wait_recv()
+    return link.send(
+        rows_of(full, shard + i * n, n), rows_of(full, 3 * shard + i * n, n), place.core
+    )
+
+
+class Scatter:
+    def __init__(self, link, place, part, core_buf, out_buf, near_buf, shard):
+        self.link, self.place, self.part = link, place, part
+        self.core_buf, self.out_buf, self.near_buf = core_buf, out_buf, near_buf
+        self.shard, self.n = shard, shard // CHUNKS
+        self.core, self.near = {}, {}
+
+    def start(self):
+        for block in (3, 2):
+            for i in range(CHUNKS):
+                at = (block - 2) * self.shard + i * self.n
+                self.core[block - 2, i] = self.link.send(
+                    rows_of(self.part, 2 * self.shard + at, self.n),
+                    rows_of(self.core_buf, at, self.n),
+                    self.place.core,
+                )
+
+    def pass_on(self, i):
+        at = self.shard + i * self.n
+        self.core[1, i].wait_recv()
+
+        @pl.loop(0, self.n // STEP)
+        def _(r):
+            here = pl.multiple_of(at + r * STEP, STEP)
+            there = pl.multiple_of(i * self.n + r * STEP, STEP)
+            total = self.part[pl.ds(here, STEP), :].astype(F32) + self.core_buf[
+                pl.ds(here, STEP), :
+            ].astype(F32)
+            self.out_buf[pl.ds(there, STEP), :] = total.astype(BF)
+
+        self.near[i] = self.link.send(
+            rows_of(self.out_buf, i * self.n, self.n),
+            rows_of(self.near_buf, i * self.n, self.n),
+            self.place.near,
+        )
+
+    def ready(self, i):
+        self.core[0, i].wait_recv()
+        self.near[i].wait_recv()
+
+    def rows(self, rows):
+        return (
+            self.part[rows, :].astype(F32)
+            + self.core_buf[rows, :].astype(F32)
+            + self.near_buf[rows, :].astype(F32)
+        )
+
+
+def scatter_scratch(shard, model):
+    return [
+        pltpu.VMEM((2 * shard, model), BF),
+        pltpu.VMEM((shard, model), BF),
+        pltpu.VMEM((shard, model), BF),
+    ]
+
+
+def over_rows(first, count, step, fn):
+    @pl.loop(0, count // step)
+    def _(r):
+        fn(pl.ds(pl.multiple_of(first + r * step, 16), step))
+
+
+class Halving:
+    def __init__(self, link, place, source, first, size, turn, work, got):
+        self.link, self.place = link, place
+        self.source, self.first, self.size = source, first, size
+        self.order = [(b + turn) % place.bits for b in range(place.bits)]
+        self.work, self.got = work, got
+        self.copies = []
+
+    def start(self, s):
+        n = self.size >> (s + 1)
+        bit = self.place.bit(self.order[s])
+        src, base = (self.source, self.first) if s == 0 else (self.work[s - 1], 0)
+        at = pl.multiple_of(base + (1 - bit) * n, 16)
+        self.copies.append(
+            self.link.send(
+                rows_of(src, at, n), self.got[s], self.place.column(1 << self.order[s])
+            )
+        )
+
+    def finish(self, s):
+        n = self.size >> (s + 1)
+        bit = self.place.bit(self.order[s])
+        src, base = (self.source, self.first) if s == 0 else (self.work[s - 1], 0)
+        self.copies[s].wait_recv()
+
+        @pl.loop(0, n // 16)
+        def _(r):
+            here = pl.multiple_of(base + bit * n + r * 16, 16)
+            to = pl.ds(pl.multiple_of(r * 16, 16), 16)
+            total = src[pl.ds(here, 16), :].astype(F32) + self.got[s][to, :].astype(F32)
+            self.work[s][to, :] = total.astype(BF)
+
+    def offset(self):
+        at, n = 0, self.size
+        for b in self.order:
+            n //= 2
+            at = at + self.place.bit(b) * n
+        return self.first + at
+
+
+def halving_scratch(size, bits, model):
+    return [pltpu.VMEM((size >> (s + 1), model), BF) for s in range(bits)]
+
+
+class Doubling:
+    def __init__(self, link, place, half, full, slice_ref, far_buf):
+        self.link, self.place, self.half, self.full = link, place, half, full
+        self.slice_ref, self.far_buf = slice_ref, far_buf
+        self.n = half.size >> place.bits
+        self.at = half.offset()
+        self.cores, self.waits = [], []
+
+    def start(self):
+        self.far = self.link.send(
+            self.slice_ref, self.far_buf, self.place.far, self.place.away
+        )
+
+    def to_core(self, at, n):
+        self.link.send(
+            rows_of(self.full, at, n), rows_of(self.full, at, n), self.place.core, self.place.home
+        )
+
+    def join(self):
+        arrive(self.far, self.place.home)
+
+        @pl.when(self.place.home)
+        def _():
+            @pl.loop(0, self.n // 16)
+            def _(r):
+                here = pl.ds(pl.multiple_of(r * 16, 16), 16)
+                to = pl.ds(pl.multiple_of(self.at + r * 16, 16), 16)
+                total = self.slice_ref[here, :].astype(F32) + self.far_buf[here, :].astype(F32)
+                self.full[to, :] = total.astype(BF)
+
+        self.block, self.count = pl.multiple_of(self.at, 16), self.n
+        self.stage = 0
+        self.push(self.block)
+
+    def push(self, fresh):
+        if self.stage < self.place.bits:
+            b = self.half.order[self.place.bits - 1 - self.stage]
+            self.copy = self.link.send(
+                rows_of(self.full, self.block, self.count),
+                rows_of(self.full, self.block, self.count),
+                self.place.column(1 << b),
+                self.place.home,
+            )
+        copy = self.link.send(
+            rows_of(self.full, fresh, self.count if self.stage == 0 else self.count // 2),
+            rows_of(self.full, fresh, self.count if self.stage == 0 else self.count // 2),
+            self.place.core,
+            self.place.home,
+        )
+        self.cores.append(copy)
+
+    def advance(self):
+        b = self.half.order[self.place.bits - 1 - self.stage]
+        bit = self.place.bit(b)
+        fresh = pl.multiple_of(self.block + (1 - 2 * bit) * self.count, 16)
+        arrive(self.copy, self.place.home)
+        self.block = pl.multiple_of(self.block - bit * self.count, 16)
+        self.count *= 2
+        self.stage += 1
+        self.push(fresh)
+
+
+def enter_kernel(
+    columns, shard, hid, cot, ids, bias, wq, wo, wu, wd,
+    full, cfull, ids_o, bias_o, wq_o, wo_o, wu_o, wd_o, send_sems, recv_sems, local_sems,
+):
+    place, link = Place(columns), Link(send_sems, recv_sems)
+    n = shard // CHUNKS
+    home, away = place.home, place.away
+    k = lax.div(place.d, 2)
+    meet([place.core, place.near, place.far, place.swap] + [place.column(m) for m in range(1, columns)])
+
+    def cut(ref, at, count):
+        return ref.at[:, pl.ds(at, count)] if len(ref.shape) == 3 else ref.at[pl.ds(at, count)]
+
+    ids_copy = link.send(ids, ids_o, place.swap, away)
+    first, near, core = {}, {}, {}
+
+    def open_gather(src, dst, key):
+        for i in range(CHUNKS):
+            first[key, i] = link.send(rows_of(src, i * n, n), rows_of(dst, i * n, n), place.swap, away)
+        for i in range(CHUNKS):
+            near[key, i] = link.make(rows_of(src, i * n, n), rows_of(dst, shard + i * n, n), place.near)
+            core[key, i] = link.make(rows_of(src, i * n, n), rows_of(dst, 2 * shard + i * n, n), place.core)
+            link.start(near[key, i], home)
+            link.start(core[key, i], home)
+
+    def second_gather(dst, key):
+        for i in range(CHUNKS):
+            arrive(first[key, i], away)
+            for copy, block, to in ((near[key, i], 1, place.near), (core[key, i], 2, place.core)):
+                again = link.make(
+                    rows_of(dst, i * n, n), rows_of(dst, block * shard + i * n, n), to, copy
+                )
+                link.start(again, away)
+
+    def relay(dst, key):
+        for i in range(CHUNKS):
+            near[key, i].wait_recv()
+            core[key, i, 1] = link.send(
+                rows_of(dst, shard + i * n, n), rows_of(dst, 3 * shard + i * n, n), place.core
+            )
+
+    def drain(key):
+        for i in range(CHUNKS):
+            core[key, i].wait_recv()
+            core[key, i, 1].wait_recv()
+
+    local = []
+
+    def keep(src, dst):
+        copy = pltpu.make_async_copy(src, dst, local_sems.at[len(local)])
+        pl.when(home)(copy.start)
+        local.append(copy)
+
+    pieces = {}
+
+    def open_weight(src, dst, key):
+        rows = src.shape[-2]
+        unit = rows // (16 * columns) * 16
+        rest = rows - unit * columns
+        if unit:
+            at = pl.multiple_of(k * unit, 16)
+            pieces[key] = link.send(cut(src, at, unit), cut(dst, at, unit), place.far, home)
+        pieces[key, 1] = None
+        if rest:
+            at = unit * columns
+            pieces[key, 1] = link.send(cut(src, at, rest), cut(dst, at, rest), place.far, home)
+
+    def share_weight(src, dst, key):
+        rows = src.shape[-2]
+        unit = rows // (16 * columns) * 16
+        pieces[key, 2] = []
+        if unit:
+            arrive(pieces[key], away)
+            at = pl.multiple_of(k * unit, 16)
+            for m in range(1, columns):
+                pieces[key, 2].append(
+                    link.send(cut(dst, at, unit), cut(dst, at, unit), place.column(m), away)
+                )
+
+    def drain_weight(key):
+        if pieces[key, 1] is not None:
+            arrive(pieces[key, 1], away)
+        for copy in pieces[key, 2]:
+            arrive(copy, away)
+
+    open_gather(hid, full, "h")
+    open_weight(wq, wq_o, "q")
+    open_weight(wo, wo_o, "o")
+    bias_copy = link.send(bias, bias_o, place.far, home)
+    open_gather(cot, cfull, "c")
+    open_weight(wu, wu_o, "u")
+    open_weight(wd, wd_o, "d")
+    keep(hid, rows_of(full, 0, shard))
+    keep(wq, wq_o)
+    keep(wo, wo_o)
+    keep(ids, ids_o)
+    keep(bias, bias_o)
+    keep(cot, rows_of(cfull, 0, shard))
+    keep(wu, wu_o)
+    keep(wd, wd_o)
+
+    second_gather(full, "h")
+    share_weight(wq, wq_o, "q")
+    share_weight(wo, wo_o, "o")
+    relay(full, "h")
+    second_gather(cfull, "c")
+    share_weight(wu, wu_o, "u")
+    relay(cfull, "c")
+    share_weight(wd, wd_o, "d")
+    drain("h")
+    drain("c")
+    for key in "qoud":
+        drain_weight(key)
+    arrive(ids_copy, away)
+    arrive(bias_copy, away)
+    for copy in local:
+        pl.when(home)(copy.wait)
+    link.close()
+
+
+def norm_stats(values):
     center = values - jnp.mean(values, axis=-1, keepdims=True)
     rstd = lax.rsqrt(jnp.mean(center * center, axis=-1, keepdims=True) + EPS)
     return center * rstd, rstd
 
 
-def norm_back(grad, hat, rstd, gain):
+def norm_pull(grad, hat, rstd, gain):
     gn = grad * gain
     return rstd * (
         gn
@@ -378,6 +668,353 @@
     )
 
 
+def mid_kernel(
+    columns, shard, part, own, vec, mid, full, core_buf, out_buf, near_buf, send_sems, recv_sems
+):
+    place, link = Place(columns), Link(send_sems, recv_sems)
+    n = shard // CHUNKS
+    meet([place.core, place.near])
+    total = Scatter(link, place, part, core_buf, out_buf, near_buf, shard)
+    total.start()
+    for i in range(CHUNKS):
+        total.pass_on(i)
+    near, core = {}, []
+    for i in range(CHUNKS):
+        total.ready(i)
+
+        def rows(here):
+            value = own[here, :].astype(F32) + total.rows(here) + vec[0:1, :]
+            mid[here, :] = value
+            full[here, :] = (norm_stats(value)[0] * vec[1:2, :] + vec[2:3, :]).astype(BF)
+
+        over_rows(i * n, n, STEP, rows)
+        near[i], copy = gather_start(link, place, full, shard, i)
+        core.append(copy)
+    for i in range(CHUNKS):
+        core.append(gather_relay(link, place, full, shard, i, near[i]))
+    for copy in core:
+        copy.wait_recv()
+    link.close()
+
+
+def back_kernel(
+    columns, shard, part, part2, grads_u, grads_d, mid, cot, vec, *refs
+):
+    place, link = Place(columns), Link(*refs[-2:])
+    bits = place.bits
+    gmid, full, out, slice_u, slice_d, sums = refs[:6]
+    scratch = list(refs[6:-2])
+    a_bufs, b_bufs = scratch[:3], scratch[3:6]
+    swap_buf = scratch[6]
+    halves = scratch[7:]
+    n = shard // CHUNKS
+    meet([place.core, place.near, place.swap] + [place.column(1 << b) for b in range(bits)])
+    total = Scatter(link, place, part, *a_bufs, shard)
+    total2 = Scatter(link, place, part2, *b_bufs, shard)
+    size = grads_u.shape[0]
+    half_u = Halving(
+        link, place, grads_u, 0, size, 0, halves[: bits - 1] + [slice_u], halves[bits - 1 : 2 * bits - 1]
+    )
+    halves = halves[2 * bits - 1 :]
+    half_d = Halving(
+        link, place, grads_d, 0, size, 1, halves[: bits - 1] + [slice_d], halves[bits - 1 : 2 * bits - 1]
+    )
+    total.start()
+    half_u.start(0)
+    half_d.start(0)
+    for i in range(CHUNKS):
+        total.pass_on(i)
+    total2.start()
+    sums[...] = jnp.zeros_like(sums)
+    near, core = {}, []
+    for i in range(CHUNKS):
+        total.ready(i)
+
+        def rows(here):
+            grad = total.rows(here)
+            out_grad = cot[here, :].astype(F32)
+            hat, rstd = norm_stats(mid[here, :])
+            value = out_grad + norm_pull(grad, hat, rstd, vec[0:1, :])
+            gmid[here, :] = value
+            full[here, :] = value.astype(BF)
+            for row, term in enumerate((value, grad * hat, grad, out_grad)):
+                sums[row : row + 1, :] += jnp.sum(term, axis=0, keepdims=True)
+
+        over_rows(i * n, n, STEP, rows)
+        near[i], copy = gather_start(link, place, full, shard, i)
+        core.append(copy)
+    for i in range(CHUNKS):
+        total2.pass_on(i)
+    for i in range(CHUNKS):
+        core.append(gather_relay(link, place, full, shard, i, near[i]))
+    for s in range(bits):
+        half_u.finish(s)
+        if s + 1 < bits:
+            half_u.start(s + 1)
+        half_d.finish(s)
+        if s + 1 < bits:
+            half_d.start(s + 1)
+    swaps = []
+    for i in range(CHUNKS):
+        total2.ready(i)
+
+        def rows2(here):
+            value = (mid[here, :] + total2.rows(here) + vec[1:2, :]).astype(BF)
+            swap_buf[here, :] = value
+
+            @pl.when(place.home)
+            def _():
+                out[here, :] = value
+
+        over_rows(i * n, n, STEP, rows2)
+        swaps.append(
+            link.send(rows_of(swap_buf, i * n, n), rows_of(out, i * n, n), place.swap, place.away)
+        )
+    for copy in core:
+        copy.wait_recv()
+    for copy in swaps:
+        arrive(copy, place.away)
+    link.close()
+
+
+def exit_kernel(
+    columns, shard, part, own, gmid, slice_u, slice_d, grads_a, small_in, vec, *refs
+):
+    place, link = Place(columns), Link(*refs[-2:])
+    bits = place.bits
+    inp, full_u, full_d, full_a, small = refs[:5]
+    scratch = list(refs[5:-2])
+    a_bufs = scratch[:3]
+    swap_buf, far_u, far_d, far_a0, far_a1 = scratch[3:8]
+    steps = bits + 3
+    sum_own, sum_got = scratch[8 : 8 + steps], scratch[8 + steps : 8 + 2 * steps]
+    halves = scratch[8 + 2 * steps :]
+    n = shard // CHUNKS
+    hops = [place.core] + [place.column(1 << b) for b in range(bits)] + [place.near, place.far]
+    meet(hops + [place.swap])
+    size = full_u.shape[0]
+    total = Scatter(link, place, part, *a_bufs, shard)
+    half_a = []
+    for side in range(2):
+        half_a.append(
+            Halving(
+                link, place, grads_a, side * (size // 2), size // 2, side,
+                halves[:bits], halves[bits : 2 * bits],
+            )
+        )
+        halves = halves[2 * bits :]
+    half_u = Halving(link, place, None, 0, size, 0, [], [])
+    half_d = Halving(link, place, None, 0, size, 1, [], [])
+    double = [
+        Doubling(link, place, half_u, full_u, slice_u, far_u),
+        Doubling(link, place, half_d, full_d, slice_d, far_d),
+        Doubling(link, place, half_a[0], full_a, half_a[0].work[bits - 1], far_a0),
+        Doubling(link, place, half_a[1], full_a, half_a[1].work[bits - 1], far_a1),
+    ]
+    total.start()
+    half_a[0].start(0)
+    half_a[1].start(0)
+    for i in range(CHUNKS):
+        total.pass_on(i)
+    double[0].start()
+    double[1].start()
+    sum_own[0][...] = small_in[...]
+    swaps = []
+    for i in range(CHUNKS):
+        total.ready(i)
+
+        def rows(here):
+            grad = total.rows(here)
+            hat, rstd = norm_stats(own[here, :].astype(F32))
+            value = (gmid[here, :] + norm_pull(grad, hat, rstd, vec[0:1, :])).astype(BF)
+            swap_buf[here, :] = value
+            for row, term in enumerate((grad * hat, grad)):
+                sum_own[0][row : row + 1, :] += jnp.sum(term, axis=0, keepdims=True)
+
+            @pl.when(place.home)
+            def _():
+                inp[here, :] = value
+
+        over_rows(i * n, n, STEP, rows)
+        swaps.append(
+            link.send(rows_of(swap_buf, i * n, n), rows_of(inp, i * n, n), place.swap, place.away)
+        )
+    hop_copies = [link.send(sum_own[0], sum_got[0], hops[0])]
+
+    def next_hop(s):
+        hop_copies[s].wait_recv()
+        into = small if s + 1 == steps else sum_own[s + 1]
+        into[...] = sum_own[s][...] + sum_got[s][...]
+        if s + 1 < steps:
+            hop_copies.append(link.send(sum_own[s + 1], sum_got[s + 1], hops[s + 1]))
+
+    hop = 0
+    for s in range(bits):
+        for half in half_a:
+            half.finish(s)
+            if s + 1 < bits:
+                half.start(s + 1)
+        if hop < steps:
+            next_hop(hop)
+            hop += 1
+    double[2].start()
+    double[3].start()
+    double[0].join()
+    double[1].join()
+    if hop < steps:
+        next_hop(hop)
+        hop += 1
+    for s in range(bits):
+        double[0].advance()
+        double[1].advance()
+        if hop < steps:
+            next_hop(hop)
+            hop += 1
+        if s == 0:
+            double[2].join()
+            double[3].join()
+    for s in range(bits):
+        double[2].advance()
+        double[3].advance()
+        if hop < steps:
+            next_hop(hop)
+            hop += 1
+    while hop < steps:
+        next_hop(hop)
+        hop += 1
+    for one in double:
+        for copy in one.cores:
+            arrive(copy, place.away)
+    for copy in swaps:
+        arrive(copy, place.away)
+    link.close()
+
+
+def any_space():
+    return pl.BlockSpec(memory_space=pl.ANY)
+
+
+SEMS = 112
+
+
+def sems():
+    return [pltpu.SemaphoreType.DMA((SEMS,)), pltpu.SemaphoreType.DMA((SEMS,))]
+
+
+def remote_call(name, kernel, number, outs, in_specs, scratch, cost=None):
+    return pl.pallas_call(
+        kernel,
+        out_shape=outs,
+        in_specs=in_specs,
+        out_specs=jax.tree.map(lambda _: vmem(), outs),
+        scratch_shapes=scratch + sems(),
+        compiler_params=pltpu.CompilerParams(
+            collective_id=number, has_side_effects=True, vmem_limit_bytes=60 << 20
+        ),
+        name=name,
+    )
+
+
+def shaped(shape, dtype):
+    return jax.ShapeDtypeStruct(shape, dtype)
+
+
+def enter(columns, hid, cot, ids, bias, wq, wo, wu, wd):
+    shard, model = hid.shape
+    outs = (
+        shaped((4 * shard, model), BF),
+        shaped((4 * shard, model), BF),
+        shaped(ids.shape, ids.dtype),
+        shaped(bias.shape, F32),
+        shaped(wq.shape, BF),
+        shaped(wo.shape, BF),
+        shaped(wu.shape, BF),
+        shaped(wd.shape, BF),
+    )
+    kernel = functools.partial(enter_kernel, columns, shard)
+    call = pl.pallas_call(
+        kernel,
+        out_shape=outs,
+        in_specs=[any_space()] * 8,
+        out_specs=tuple(vmem() for _ in outs),
+        scratch_shapes=[
+            pltpu.SemaphoreType.DMA((48 + 6 * columns,)),
+            pltpu.SemaphoreType.DMA((48 + 6 * columns,)),
+            pltpu.SemaphoreType.DMA((8,)),
+        ],
+        compiler_params=pltpu.CompilerParams(
+            collective_id=0, has_side_effects=True, vmem_limit_bytes=60 << 20
+        ),
+        name="enter",
+    )
+    return call(hid, cot, ids, bias, wq, wo, wu, wd)
+
+
+def make_mid(columns, part, own, vec):
+    shard, model = own.shape
+    outs = (shaped((shard, model), F32), shaped((4 * shard, model), BF))
+    call = remote_call(
+        "mid", functools.partial(mid_kernel, columns, shard), 1, outs, [vmem()] * 3,
+        scatter_scratch(shard, model),
+    )
+    return call(part, own, vec)
+
+
+def make_back(columns, part, part2, grads_u, grads_d, mid, cot, vec):
+    shard, model = mid.shape
+    bits = columns.bit_length() - 1
+    size = grads_u.shape[0]
+    outs = (
+        shaped((shard, model), F32),
+        shaped((4 * shard, model), BF),
+        shaped((shard, model), BF),
+        shaped((size // columns, model), BF),
+        shaped((size // columns, model), BF),
+        shaped((8, model), F32),
+    )
+    per_side = halving_scratch(size, bits, model)
+    halves = per_side[: bits - 1] + per_side
+    call = remote_call(
+        "back", functools.partial(back_kernel, columns, shard), 2, outs, [vmem()] * 7,
+        scatter_scratch(shard, model)
+        + scatter_scratch(shard, model)
+        + [pltpu.VMEM((shard, model), BF)]
+        + halves
+        + halves,
+    )
+    return call(part, part2, grads_u, grads_d, mid, cot, vec)
+
+
+def make_exit(columns, part, own, gmid, slice_u, slice_d, grads_a, small, vec):
+    shard, model = own.shape
+    bits = columns.bit_length() - 1
+    size = grads_a.shape[0]
+    outs = (
+        shaped((shard, model), BF),
+        shaped((size, model), BF),
+        shaped((size, model), BF),
+        shaped((size, model), BF),
+        shaped(small.shape, F32),
+    )
+    n = size // columns
+    per_side = halving_scratch(size // 2, bits, model)
+    steps = bits + 3
+    call = remote_call(
+        "exit", functools.partial(exit_kernel, columns, shard), 3, outs, [vmem()] * 8,
+        scatter_scratch(shard, model)
+        + [
+            pltpu.VMEM((shard, model), BF),
+            pltpu.VMEM((n, model), BF),
+            pltpu.VMEM((n, model), BF),
+            pltpu.VMEM((n // 2, model), BF),
+            pltpu.VMEM((n // 2, model), BF),
+        ]
+        + [pltpu.VMEM(small.shape, F32)] * (2 * steps)
+        + (per_side + per_side) * 2,
+    )
+    return call(part, own, gmid, slice_u, slice_d, grads_a, small, vec)
+
+
 def mm(a, b):
     return jnp.dot(a, b, preferred_element_type=F32)
 
@@ -388,6 +1025,12 @@
 
 def mm_tn(a, b):
     return lax.dot_general(a, b, (((0,), (0,)), ((), ())), preferred_element_type=F32)
+
+
+def stack_rows(rows, model):
+    rows = [jnp.pad(r, (0, model - r.shape[0])) for r in rows]
+    rows = rows + [jnp.zeros((model,), F32)] * (-len(rows) % 8)
+    return jnp.stack(rows)
 
 
 def body(
@@ -411,52 +1054,34 @@
     _, shard, model = hidden.shape
     seq = segment_ids.shape[1]
     width = qkv_weight.shape[2]
-    hidden_units = up_weight.shape[1]
     d, t = lax.axis_index("dp"), lax.axis_index("tensor")
     columns = lax.axis_size("dp") // 2
-    column = d >> 1
-    home = is_home(d, t)
     rank = 2 * (d & 1) + (t & 1)
 
-    own = send(hidden[0], swap_rule)
-    full = gather4(own)
-    ids = jnp.concatenate([segment_ids[0], lengths])
-    ids = send(ids, swap_rule)
-    length = ids[seq]
+    ids = jnp.concatenate([segment_ids[0], lengths, jnp.zeros((LANES - 1,), jnp.int32)])
+    ids = jnp.broadcast_to(ids[None], (8, seq + LANES))
+    bias = jnp.broadcast_to(jnp.concatenate([qv_bias.reshape(-1), up_bias])[None], (8, 2 * width + up_bias.shape[0]))
+    full, cot_full, ids, bias, w_qkv, w_out, w_up, w_down = enter(
+        columns, hidden[0], cotangent[0], ids, bias, qkv_weight, out_weight, up_weight, down_weight
+    )
+    length = ids[0, seq]
     places = jnp.arange(seq, dtype=jnp.int32)
-    ids = jnp.where(places < length, ids[:seq], 16 + places)
+    ids = jnp.where(places < length, ids[0, :seq], 16 + places)
     start = jnp.sum((ids[None, :] < ids[:, None]).astype(jnp.int32), axis=1)
     meta = jnp.concatenate([rank[None], start[::BLK] // BLK]).astype(jnp.int32)
     start = start[None, :]
-
-    w_qkv = spread_weight(
-        jnp.concatenate([qkv_weight[0], qkv_weight[1], qkv_weight[2]], axis=0), home, column, columns
-    ).reshape(3, model, width)
-    bias = jnp.concatenate([qv_bias.reshape(-1), up_bias])
-    far_bias = send(bias, lambda d, t: (d, t ^ 2) if is_home(d, t) else None)
-    bias = jnp.where(home, bias, far_bias)
-    b_q, b_v, b_up = bias[:width], bias[width : 2 * width], bias[2 * width :]
-
-    cot, own, up_w, down_w, out_w = lax.optimization_barrier(
-        (cotangent[0], own, up_weight, down_weight, out_weight)
-    )
-    w_out = spread_weight(out_w, home, column, columns)
-    w_up = spread_weight(up_w, home, column, columns)
-    w_down = spread_weight(down_w, home, column, columns)
-    cot_own = send(cot, swap_rule)
-    cot_full = gather4(cot_own)
-
-    resid_full = full.astype(F32)
-    hat1, rstd1 = norm_parts(resid_full)
-    normed1 = (hat1 * norm1_gain + norm1_shift).astype(BF)
+    b_q, b_v, b_up = bias[0, :width], bias[0, width : 2 * width], bias[0, 2 * width :]
+    own, cot_own = full[:shard], cot_full[:shard]
+
+    normed1 = (norm_stats(full.astype(F32))[0] * norm1_gain + norm1_shift).astype(BF)
     q = (mm(normed1, w_qkv[0]) + b_q).astype(BF)
     k = mm(normed1, w_qkv[1]).astype(BF)
     v = (mm(normed1, w_qkv[2]) + b_v).astype(BF)
     attended, lse = attn_fwd(meta, start, q, k, v, shard)
 
-    mid = own.astype(F32) + scatter4(mm(attended, w_out)) + out_bias
-    hat2, rstd2 = norm_parts(mid)
-    normed2 = gather4((hat2 * norm2_gain + norm2_shift).astype(BF))
+    mid, normed2 = make_mid(
+        columns, mm(attended, w_out).astype(BF), own, stack_rows([out_bias, norm2_gain, norm2_shift], model)
+    )
     inner = mm(normed2, w_up) + b_up
     c0 = math.sqrt(2.0 / math.pi)
     tanh = jnp.tanh(c0 * (inner + 0.044715 * inner * inner * inner))
@@ -465,70 +1090,69 @@
         1.0 + 3 * 0.044715 * inner * inner
     )
     grad_inner = (mm_nt(cot_full, w_down) * slope).astype(BF)
-    grad_normed2 = scatter4(mm_nt(grad_inner, w_up))
-    grad_out = cot_own.astype(F32)
-    grad_mid = grad_out + norm_back(grad_normed2, hat2, rstd2, norm2_gain)
-    gm_full = gather4(grad_mid.astype(BF))
-
-    output = mid + scatter4(mm(active, w_down)) + down_bias
-    output = send(output.astype(BF), swap_rule)
-    up_grad = mm_tn(normed2, grad_inner).astype(BF)
-    down_grad = mm_tn(active, cot_full).astype(BF)
-    mlp_grad = reduce_grad(jnp.concatenate([up_grad, down_grad], axis=0), home, column, columns)
-
+    unit = 32 * columns
+    pad = -model % unit
+    up_grad = jnp.pad(mm_tn(normed2, grad_inner).astype(BF), ((0, pad), (0, 0)))
+    down_grad = jnp.pad(mm_tn(active, cot_full).astype(BF), ((0, pad), (0, 0)))
+    grad_mid, gm_full, output, slice_u, slice_d, sums = make_back(
+        columns,
+        mm_nt(grad_inner, w_up).astype(BF),
+        mm(active, w_down).astype(BF),
+        up_grad,
+        down_grad,
+        mid,
+        cot_own,
+        stack_rows([norm2_gain, down_bias], model),
+    )
     grad_attended = mm_nt(gm_full, w_out).astype(BF)
-    out_grad = reduce_grad(mm_tn(attended, gm_full).astype(BF), home, column, columns)
     dq, dk, dv = attn_bwd(meta, start, q, k, v, attended, grad_attended, lse, shard)
     part1 = mm_nt(dq, w_qkv[0]) + mm_nt(dk, w_qkv[1]) + mm_nt(dv, w_qkv[2])
-    grad_normed1 = scatter4(part1)
-    hat1_own, rstd1_own = norm_parts(own.astype(F32))
-    input_grad = grad_mid + norm_back(grad_normed1, hat1_own, rstd1_own, norm1_gain)
-    input_grad = send(input_grad.astype(BF), swap_rule)
-    qkv_grad = jnp.concatenate(
-        [mm_tn(normed1, dq), mm_tn(normed1, dk), mm_tn(normed1, dv)], axis=0
+    att_grad = jnp.concatenate(
+        [mm_tn(dq, normed1), mm_tn(dk, normed1), mm_tn(dv, normed1), mm_tn(attended, gm_full)], axis=0
     ).astype(BF)
-    qkv_grad = reduce_grad(qkv_grad, home, column, columns).reshape(3, model, width)
-
-    quarter_bias = jnp.concatenate(
-        [
-            jnp.sum(dq, axis=0, dtype=F32),
-            jnp.sum(dv, axis=0, dtype=F32),
-            jnp.sum(grad_inner, axis=0, dtype=F32),
-        ]
-    )
+    att_grad = jnp.pad(att_grad, ((0, pad), (0, 0)))
+
+    qv_grad = jnp.concatenate([jnp.sum(dq, axis=0, dtype=F32), jnp.sum(dv, axis=0, dtype=F32)])
+    qv_grad = jnp.pad(qv_grad, (0, model - 2 * width))
+    up_b_grad = jnp.sum(grad_inner, axis=0, dtype=F32)
     slots = lax.broadcasted_iota(jnp.int32, (4, 1), 0) == rank
     small = jnp.concatenate(
         [
-            jnp.sum(part1 * hat1, axis=0),
-            jnp.sum(part1, axis=0),
-            jnp.sum(grad_mid, axis=0),
-            jnp.sum(grad_normed2 * hat2, axis=0),
-            jnp.sum(grad_normed2, axis=0),
-            jnp.sum(grad_out, axis=0),
-            jnp.where(slots, quarter_bias[None], 0.0).reshape(-1),
+            jnp.zeros((2, model), F32),
+            sums[:4],
+            jnp.zeros((2, model), F32),
+            jnp.where(slots, up_b_grad[None], 0.0),
+            jnp.where(slots, qv_grad[None], 0.0),
         ]
     )
-    small = sum_all(small)
-    gain1, shift1, out_b, gain2, shift2, down_b = [
-        small[i * model : (i + 1) * model] for i in range(6)
-    ]
-    split = 2 * width + hidden_units
-    quarter = lax.dynamic_slice_in_dim(small, 6 * model + t * split, split, 0)
+    input_grad, up_grad, down_grad, att_grad, small = make_exit(
+        columns,
+        part1.astype(BF),
+        own,
+        grad_mid,
+        slice_u,
+        slice_d,
+        att_grad,
+        small,
+        stack_rows([norm1_gain], model),
+    )
+    quarter = lax.dynamic_slice_in_dim(small, 12 + t, 1, 0)[0, : 2 * width].reshape(2, width)
+    qkv_grad = att_grad[: 3 * width].reshape(3, width, model).astype(F32)
     return (
         output[None],
         input_grad[None],
-        gain1,
-        shift1,
-        qkv_grad,
-        quarter[: 2 * width].reshape(2, width),
-        out_grad,
-        out_b,
-        gain2,
-        shift2,
-        mlp_grad[:model],
-        quarter[2 * width :],
-        mlp_grad[model:],
-        down_b,
+        small[0],
+        small[1],
+        jnp.swapaxes(qkv_grad, 1, 2),
+        quarter,
+        att_grad[3 * width : 4 * width].astype(F32),
+        small[2],
+        small[3],
+        small[4],
+        up_grad[:model].astype(F32),
+        lax.dynamic_slice_in_dim(small, 8 + t, 1, 0)[0],
+        down_grad[:model].astype(F32),
+        small[5],
     )
 
 

time: 725 us -> 536 us (0.74)
  Pallas kernels: 37.6 us -> 381 us
  starting transfers between devices: 161 us -> 0 us
  waiting for transfers between devices: 137 us -> 0 us
  local copies, waits for them, and re-layouts: 172 us -> 49.9 us
  other arithmetic: 119 us -> 30 us
  matrix products: 81.7 us -> 66.4 us
    pallas_call x0 -> x4, Pallas kernels: none -> 344 us  [the longest x1 117 us: enter(): return call(hid, cot, ids, bias, wq, wo, wu, wd)]
    ppermute x80 -> x0, starting transfers between devices: 161 us -> none  [send(): return lax.ppermute(x, AXES, pairs)]
    ppermute x80 -> x0, waiting for transfers between devices: 137 us -> none  [send(): return lax.ppermute(x, AXES, pairs)]
    ppermute x15 -> x0, local copies, waits for them, and re-layouts: 31.3 us -> none  [send(): return lax.ppermute(x, AXES, pairs)]
    convert_element_type x28 -> x4, other arithmetic: 39.7 us -> 9.23 us  [the longest x1 2.66 us: body(): up_grad[:model].astype(F32)]
    concatenate x9 -> x2, local copies, waits for them, and re-layouts: 31.2 us -> 1.36 us  [the longest x1 1.28 us: body(): jnp.concatenate([jnp.zeros((2, model), F32), sums[:4], jnp.zeros((2, mode...]
    dynamic_update_slice x4 -> x0, local copies, waits for them, and re-layouts: 24.7 us -> none  [spread_weight(): lax.dynamic_update_slice_in_dim(whole, jnp.where(home, piece(index), got)...]
    dynamic_update_slice x12 -> x0, other arithmetic: 21.9 us -> none  [spread_weight(): lax.dynamic_update_slice_in_dim(whole, jnp.where(home, piece(index), got)...]
  transfers between devices with their start and end apart: 80 -> 0, of which waited for: 20 -> 0; matrix products, arithmetic and copies ran while one was open for 44% -> 0% of each run, Pallas kernels for 5% -> 0%
where the time goes in v2:
time: 536 us; the launch traced here: 529 us
  Pallas kernels  381 us (71%)
  matrix products  66.4 us (12%)
  local copies, waits for them, and re-layouts  49.9 us (9%)
  other arithmetic  30 us (6%)
    pallas_call x1, Pallas kernels, enter(): return call(hid, cot, ids, bias, wq, wo, wu, wd)  117 us
    pallas_call x1, Pallas kernels, make_exit(): return call(part, own, gmid, slice_u, slice_d, grads_a, small, vec)  98.4 us
    pallas_call x1, Pallas kernels, make_back(): return call(part, part2, grads_u, grads_d, mid, cot, vec)  85.7 us
    pallas_call x1, Pallas kernels, make_mid(): return call(part, own, vec)  42.3 us
    dot_general x6, matrix products, mm_nt(): lax.dot_general(a, b, (((1,), (1,)), ((), ())), preferred_element_type=F32)  28.3 us
    dot_general x6, matrix products, mm(): return jnp.dot(a, b, preferred_element_type=F32)  22 us
    pallas_call x1, Pallas kernels, attn_bwd(): pl.pallas_call(functools.partial(attn_bwd_kernel, heads, shard), out_shap...  21.7 us
    dot_general x6, matrix products, mm_tn(): lax.dot_general(a, b, (((0,), (0,)), ((), ())), preferred_element_type=F32)  16 us

profile of v2, /device:TPU:1, one launch (start us, length us, event | category | flops | bytes accessed | tf_op | source)
XLA Modules:
  0.0 529.3 jit_solution(9587046996913368758)
XLA Ops:
  1.3 0.8 reshape.81
  2.1 0.8 pad_maximum_fusion.4
  2.8 0.7 stack.24
  3.5 0.7 stack.23
  4.2 0.7 stack.25
  4.9 0.7 stack.27
  5.6 0.7 broadcast_in_dim.73
  6.3 0.7 reduce
  9.7 4.1 copy.56.wq
  13.9 117.3 %enter.1 = (bf16[1280,1120]{1,0:T(8,128)(2,1)}, bf16[1280,1120]{1,0:T(8,128)(2,1)}, s32[8,1408]{1,0:T(8,128)}, f32[8,1680]{1,0:T(8,128)}, bf16[3,1120,280]{2,1,0...) custom-call(bf16[320,1120]{1,0:T(8,128)(2,1)} %bitcast.56, ...), custom_call_target="tpu_custom_call" | custom-call | tf_op jit(solution)/shard_map/enter/pallas_call | solution.py:950
  131.2 1.3 slice.72
  132.5 0.9 slice_reduce_fusion.8
  133.4 0.9 slice_reduce_fusion.6
  134.3 2.3 convert_reduce_fusion
  136.6 0.9 fusion.4
  137.6 1.5 slice_reduce_fusion.7
  139.7 0.8 convert_reduce_fusion.1
  141.8 0.9 slice.80.own
  142.7 1.7 fusion.7
  144.4 2.6 slice.82.cot
  147.0 2.8 fusion.18.v
  149.8 2.7 fusion.17.q
  152.6 2.7 convolution_convert_fusion.5.k
  155.3 15.5 %attn_fwd.1 = (bf16[1280,280]{1,0:T(8,128)(2,1)}, f32[8,1280]{1,0:T(8,128)}) custom-call(s32[6]{0:T(128)} %pad_add_fusion.meta, s32[1,1280]{1,0:T(1,128)} %broadcast_in_dim.68.start, bf16[1280,280]{1,0:T(8,128)(2,1)} %fusion.17.q, bf16[1280,280]{1,0:T(8,128)(2,1)} %convolution_convert_fusion.5.k, bf16[1280,280]{1,0:T(8,128)(2,1)} %fusion.18.v), custom_call_target="tpu_custom_call" | custom-call | flops 1376256000 | bytes 5734400 | tf_op jit(solution)/shard_map/attn_fwd/pallas_call | solution.py:209
  170.8 3.1 convolution_convert_fusion.2
  173.9 3.3 copy.60.part
  177.2 42.3 %mid.1 = (f32[320,1120]{1,0:T(8,128)}, bf16[1280,1120]{1,0:T(8,128)(2,1)}) custom-call(bf16[1280,1120]{1,0:T(8,128)(2,1)} %copy.60.part, bf16[320,1120]{1,0:T(8,128)(2,1)} %slice.80.own, f32[8,1120]{1,0:T(8,128)} %stack.26.vec), custom_call_target="tpu_custom_call" | custom-call | tf_op jit(solution)/shard_map/mid/pallas_call | solution.py:960
  219.5 6.3 %convolution_add_fusion.2 = f32[1280,1120]{0,1:T(8,128)S(1)} fusion(bf16[1280,1120]{1,0:T(8,128)(2,1)} %get-tuple-element.48, bf16[1120,1120]{1,0:T(8,128)(2,1)S(1)} %copy-done.17, f32[1120]{0:T(1024)S(1)} %slice_reduce_fusion.6), kind=kOutput, calls=%fused_computation.3 | convolution fusion | flops 3212697600 | bytes 11114880 | tf_op jit(solution)/shard_map/dot_general | solution.py:1019
  225.8 5.1 convolution_convert_fusion
  230.9 6.6 %convert_reduce_fusion.2 = (f32[1120]{0:T(1024)S(1)}, bf16[1280,1120]{0,1:T(8,128)(2,1)S(1)}) fusion(f32[1280,1120]{0,1:T(8,128)S(1)} %convolution_add_fusion.2, bf16[1280,1120]{1,0:T(8,128)(2,1)S(1)} %copy-done.12, bf16[1120,1120]{1,0:T(8,128)(2,1)S(1)} %copy-done.18), kind=kOutput, calls=%fused_computation.27 | convolution fusion | flops 3241368576 | bytes 13982080 | tf_op jit(solution)/shard_map/dot_general | solution.py:1023
  237.5 4.4 convolution_convert_fusion.4
  241.9 4.1 convolution_convert_fusion.1
  246.0 1.7 pad.14.grads_u
  247.7 1.7 pad.15.grads_d
  249.5 3.3 copy.64.part2
  252.7 6.5 %convolution_convert_fusion.3 = bf16[1280,1120]{0,1:T(8,128)(2,1)S(1)} fusion(bf16[1120,1120]{1,0:T(8,128)(2,1)} %get-tuple-element.49, bf16[1280,1120]{0,1:T(8,128)(2,1)} %copy-done.21), kind=kOutput, calls=%fused_computation.11 | convolution fusion | flops 3212697600 | bytes 8243200 | tf_op jit(solution)/shard_map/dot_general | solution.py:1023
  259.2 3.5 copy.63.part
  262.7 85.7 %back.1 = (f32[320,1120]{1,0:T(8,128)}, bf16[1280,1120]{1,0:T(8,128)(2,1)}, bf16[320,1120]{1,0:T(8,128)(2,1)}, bf16[288,1120]{1,0:T(8,128)(2,1)}, bf16[288,1120]{1,0:T(8,128)(2,1)}, /*index=5*/f32[8,1120]{1,0:T(8,128)}) custom-call(bf16[1280,1120]{1,0:T(8,128)(2,1)} %copy.63.part, bf16[1280,1120]{1,0:T(8,128)(2,1)} %copy.64.part2, ...), custom_call_target="tpu_custom_call" | custom-call | tf_op jit(solution)/shard_map/back/pallas_call | solution.py:985
  348.5 0.8 slice.83
  349.2 3.1 convolution_convert_fusion.6
  352.4 1.1 convolution_convert_fusion.7
  353.5 1.3 copy.65.do
  354.8 21.7 %attn_bwd.1 = (bf16[1280,280]{1,0:T(8,128)(2,1)}, bf16[1280,280]{1,0:T(8,128)(2,1)}, bf16[1280,280]{1,0:T(8,128)(2,1)}) custom-call(s32[6]{0:T(128)} %pad_add_fusion.meta, s32[1,1280]{1,0:T(1,128)} %broadcast_in_dim.68.start, bf16[1280,280]{1,0:T(8,128)(2,1)} %fusion.17.q, bf16[1280,280]{1,0:T(8,128)(2,1)} %convolution_convert_fusion.5.k, ...), custom_call_target="tpu_custom_call" | custom-call | flops 3670016000 | bytes 5734400 | tf_op jit(solution)/shard_map/attn_bwd/pallas_call | solution.py:238
  376.5 1.8 convert_reduce_fusion.3
  378.5 1.3 concatenate.24.small_in
  379.8 3.4 convolution_convert_fusion.9
  383.2 1.2 convolution_convert_fusion.10
  384.4 1.2 convolution_convert_fusion.8
  385.6 7.7 %fusion.21.grads_a = bf16[1152,1120]{1,0:T(8,128)(2,1)} fusion(bf16[280,1120]{1,0:T(8,128)(2,1)S(1)} %convolution_convert_fusion.7, bf16[280,1120]{1,0:T(8,128)(2,1)S(1)} %convolution_convert_fusion.8, bf16[280,1120]{1,0:T(8,128)(2,1)S(1)} %convolution_convert_fusion.9, bf16[280,1120]{1,0:T(8,128)(2,1)S(1)} %convolution_convert_fusion.10), kind=kLoop, calls=%fused_computation.42 | loop fusion | flops 16773120 | bytes 5089280 | tf_op jit(solution)/shard_map/concatenate | solution.py:1110
  393.3 1.7 fusion.26
  395.0 4.2 convolution_add_fusion
  399.2 7.6 %copy.66 = f32[1280,1120]{1,0:T(8,128)} copy(f32[1280,1120]{0,1:T(8,128)} %convolution_add_fusion) | data formatting | bytes 11468800 | tf_op jit(solution)/shard_map/add | solution.py:1109
  406.8 6.3 %fusion.1.part = bf16[1280,1120]{1,0:T(8,128)(2,1)} fusion(f32[1280,1120]{1,0:T(8,128)} %copy.66, bf16[1280,280]{1,0:T(8,128)(2,1)S(1)} %copy-done.2, bf16[3,1120,280]{2,1,0:T(8,128)(2,1)} %get-tuple-element.44), kind=kOutput, calls=%fused_computation.10 | convolution fusion | flops 805683200 | bytes 10342400 | tf_op jit(solution)/shard_map/dot_general | solution.py:1023
  413.1 98.4 %exit.1 = (bf16[320,1120]{1,0:T(8,128)(2,1)}, bf16[1152,1120]{1,0:T(8,128)(2,1)}, bf16[1152,1120]{1,0:T(8,128)(2,1)}, bf16[1152,1120]{1,0:T(8,128)(2,1)}, f32[16,1120]{1,0:T(8,128)}) custom-call(bf16[1280,1120]{1,0:T(8,128)(2,1)} %fusion.1.part, bf16[320,1120]{1,0:T(8,128)(2,1)} %slice.80.own, f32[320,1120]{1,0:T(8,128)} %get-tuple-element.57.gmid, ...), custom_call_target="tpu_custom_call" | custom-call | tf_op jit(solution)/shard_map/exit/pallas_call | solution.py:1015
  511.5 0.8 dynamic-slice_reduce_fusion.1
  512.3 1.7 slice_reduce_fusion
  514.6 2.2 slice_convert_fusion.2
  516.9 1.7 slice.86
  518.6 2.2 convert_bitcast_fusion
  520.7 0.9 copy-done.9
  521.6 2.7 slice_convert_fusion.1
  524.5 2.7 slice_convert_fusion
  527.1 0.9 copy.77
  528.0 0.9 copy.78
  (63 shorter events, 5.8 us)
Async XLA Ops:
  131.2 5.4 %copy-start = (bf16[1280,1120]{1,0:T(8,128)(2,1)S(1)}, bf16[1280,1120]{1,0:T(8,128)(2,1)}, u32[]{:S(2)}) copy-start(bf16[1280,1120]{1,0:T(8,128)(2,1)} %get-tuple-element.43) | copy-start | bytes 8601604
  136.6 6.1 %copy-start.13 = (f32[1120]{0:T(1024)S(1)}, f32[1120]{0:T(1024)}, u32[]{:S(2)}) copy-start(f32[1120]{0:T(1024)} %param.19) | copy-start | bytes 13444
  136.6 6.1 %copy-start.14 = (f32[1120]{0:T(1024)S(1)}, f32[1120]{0:T(1024)}, u32[]{:S(2)}) copy-start(f32[1120]{0:T(1024)} %param.20) | copy-start | bytes 13444
  142.7 4.3 copy-start.6
  144.4 8.1 %copy-start.4 = (bf16[1280,1120]{1,0:T(8,128)(2,1)}, bf16[1280,1120]{1,0:T(8,128)(2,1)S(1)}, u32[]{:S(2)}) copy-start(bf16[1280,1120]{1,0:T(8,128)(2,1)S(1)} %fusion.7) | copy-start | bytes 8601604
  177.2 42.3 %copy-start.17 = (bf16[1120,1120]{1,0:T(8,128)(2,1)S(1)}, bf16[1120,1120]{1,0:T(8,128)(2,1)}, u32[]{:S(2)}) copy-start(bf16[1120,1120]{1,0:T(8,128)(2,1)} %get-tuple-element.49) | copy-start | bytes 7526404
  219.5 6.3 %copy-start.12 = (bf16[1280,1120]{1,0:T(8,128)(2,1)S(1)}, bf16[1280,1120]{1,0:T(8,128)(2,1)}, u32[]{:S(2)}) copy-start(bf16[1280,1120]{1,0:T(8,128)(2,1)} %get-tuple-element.40) | copy-start | bytes 8601604
  225.8 5.1 copy-start.18
  237.5 4.4 copy-start.21
  237.5 4.4 copy-start.16
  262.7 86.5 %copy-start.19 = (bf16[280,1120]{1,0:T(8,128)(2,1)S(1)}, bf16[280,1120]{1,0:T(8,128)(2,1)}, u32[]{:S(2)}) copy-start(bf16[280,1120]{1,0:T(8,128)(2,1)} %get-tuple-element.47) | copy-start | bytes 1881604
  349.2 3.1 copy-start.15
  349.2 3.2 copy-start.20
  378.3 4.9 copy-start.1
  379.8 3.4 copy-start.5
  383.2 1.2 copy-start.2
  385.6 7.7 %copy-start.7 = (bf16[3,1120,280]{2,1,0:T(8,128)(2,1)S(1)}, bf16[3,1120,280]{2,1,0:T(8,128)(2,1)}, u32[]{:S(2)}) copy-start(bf16[3,1120,280]{2,1,0:T(8,128)(2,1)} %get-tuple-element.44) | copy-start | bytes 5644804
  393.3 1.7 copy-start.3
  518.5 3.1 copy-start.9
  521.6 2.9 copy-start.8
  524.5 2.7 copy-start.10
  524.5 3.5 copy-start.11
